TPU v7x, 32 devices: a whole 2x2x4 slice. The times are simulated.
32 devices in a mesh: ctx: 8 (over z, core), head: 4 (over y, x).
Axes of the slice: x: 2, y: 2, z: 4, core: 2. Of those that a mesh axis runs over, the one named last changes fastest.
Arguments:
- queries: bfloat16 [3072, 32, 128], P(('ctx', 'head')), may hold values from -52 to 52
- key_vectors: bfloat16 [3072, 32, 128], P(('ctx', 'head')), may hold values from -4 to 4
- values: bfloat16 [3072, 32, 128], P(('ctx', 'head')), may hold values from -6 to 6
- directions: bfloat16 [3072, 32, 128], P(('ctx', 'head')), may hold values from -6 to 6
- beta_logit: bfloat16 [3072, 32], P(('ctx', 'head')), may hold values from -4.5 to 9
Outputs:
- attended: bfloat16 [3072, 32, 128], P(('ctx', 'head'))
All inputs are finite; a program needn't handle non-finite values.
Results may differ from a plain program's by a relative error of at most 0.0052.
Values may be sent and summed in bfloat16 or wider, within the bound.
A program may use at most 64 MiB of HBM per device.

v0:
```python
import jax
import jax.numpy as jnp
from jax import lax
from jax.sharding import PartitionSpec as P

SUB = 64


precise = lax.Precision.HIGHEST
far_below = -1e30


def from_behind(value, axis, by):
    length = lax.axis_size(axis)
    pairs = [(i, i + by) for i in range(length) if 0 <= i + by < length]
    return lax.ppermute(value, axis, pairs)


def unit_rows(directions):
    widened = directions.astype(jnp.float32)
    return widened * lax.rsqrt(jnp.sum(widened * widened, axis=-1, keepdims=True) + 1e-06)


def sub_blocks(query_float, key_float, unit_dirs, beta_rate, sub_size):
    row_count, head_count, head_width = query_float.shape
    sub_count = row_count // sub_size
    query_sub = query_float.reshape(sub_count, sub_size, head_count, head_width)
    key_sub = key_float.reshape(sub_count, sub_size, head_count, head_width)
    dir_sub = unit_dirs.reshape(sub_count, sub_size, head_count, head_width)
    rate_sub = beta_rate.reshape(sub_count, sub_size, head_count)
    positions = lax.iota(jnp.int32, sub_size)
    strictly_lower = positions[:, None] > positions[None, :]
    lower_incl = positions[:, None] >= positions[None, :]
    identity_sub = jnp.eye(sub_size, dtype=jnp.float32)
    gram_matrix = jnp.einsum("nahe,nbhe->nhab", dir_sub, dir_sub, precision=precise)
    inv_rate = jnp.transpose(1.0 / rate_sub, (0, 2, 1))
    triangle = jnp.where(strictly_lower, gram_matrix, 0.0) + identity_sub * inv_rate[..., None]
    inverse = jax.scipy.linalg.solve_triangular(
        triangle, jnp.broadcast_to(identity_sub, triangle.shape), lower=True
    )
    query_dots = jnp.where(
        lower_incl, jnp.einsum("nihe,nahe->nhia", query_sub, dir_sub, precision=precise), 0.0
    )
    key_dots = jnp.where(
        strictly_lower.T, jnp.einsum("njhe,nbhe->nhjb", key_sub, dir_sub, precision=precise), 0.0
    )
    query_mix = jnp.einsum("nhia,nhab->nhib", query_dots, inverse, precision=precise)
    key_mix = jnp.einsum("nhjb,nhab->nhja", key_dots, inverse, precision=precise)
    inner_scores = jnp.einsum(
        "nihe,njhe->nhij", query_sub, key_sub, precision=precise
    ) - jnp.einsum("nhib,nhjb->nhij", query_mix, key_dots, precision=precise)
    start_query = query_sub - jnp.einsum("nhib,nbhe->nihe", query_mix, dir_sub, precision=precise)
    end_keys = key_sub - jnp.einsum("nhja,nahe->njhe", key_mix, dir_sub, precision=precise)
    transport = jnp.eye(head_width, dtype=jnp.float32) - jnp.einsum(
        "nahe,nhab,nbhf->nhef", dir_sub, inverse, dir_sub, precision=precise
    )
    return (inner_scores, start_query, end_keys, transport)


def frames(inner_scores, start_query, end_keys, transport, sub_size, score_scale):
    sub_count, _, head_count, head_width = start_query.shape
    frame_count = sub_count // 2
    frame_size = 2 * sub_size
    inner_pairs = inner_scores.reshape(frame_count, 2, head_count, sub_size, sub_size)
    query_pairs = start_query.reshape(frame_count, 2, sub_size, head_count, head_width)
    key_pairs = end_keys.reshape(frame_count, 2, sub_size, head_count, head_width)
    map_pairs = transport.reshape(frame_count, 2, head_count, head_width, head_width)
    first_map = map_pairs[:, 0]
    second_map = map_pairs[:, 1]
    lifted_query = jnp.einsum("fihe,fhek->fihk", query_pairs[:, 1], first_map, precision=precise)
    pushed_keys = jnp.einsum("fjhk,fhek->fjhe", key_pairs[:, 0], second_map, precision=precise)
    framed_query_rows = jnp.concatenate([query_pairs[:, 0], lifted_query], axis=1)
    frame_keys = jnp.concatenate([pushed_keys, key_pairs[:, 1]], axis=1)
    frame_map = jnp.einsum("fhek,fhkg->fheg", second_map, first_map, precision=precise)
    cross_scores = jnp.einsum(
        "fihe,fjhe->fhij", query_pairs[:, 1], key_pairs[:, 0], precision=precise
    )
    blocked = jnp.zeros_like(cross_scores)
    upper_half = jnp.concatenate([inner_pairs[:, 0], blocked], axis=-1)
    lower_half = jnp.concatenate([cross_scores, inner_pairs[:, 1]], axis=-1)
    combined_parts = jnp.concatenate([upper_half, lower_half], axis=2) * score_scale
    positions = lax.iota(jnp.int32, frame_size)
    combined_parts = jnp.where(positions[:, None] >= positions[None, :], combined_parts, far_below)
    return (combined_parts, framed_query_rows, frame_keys, frame_map)


def start_state(combined_parts, frame_values):
    frame_count, head_count, frame_size, _ = combined_parts.shape
    row_maximum = jnp.max(combined_parts, axis=-1)
    weights = jnp.exp(combined_parts - row_maximum[..., None])
    row_total = jnp.sum(weights, axis=-1)
    weighted = jnp.einsum(
        "fhij,fjhe->fihe",
        weights.astype(jnp.bfloat16),
        frame_values,
        preferred_element_type=jnp.float32,
    )
    row_count = frame_count * frame_size
    row_maximum = jnp.transpose(row_maximum, (0, 2, 1)).reshape(row_count, head_count)
    row_total = jnp.transpose(row_total, (0, 2, 1)).reshape(row_count, head_count)
    weighted = weighted.reshape(row_count, head_count, weighted.shape[-1])
    return (row_maximum, row_total, weighted)


def absorb(softmax_state, scores, value_entries):
    row_maximum, row_total, weighted = softmax_state
    new_max = jnp.maximum(row_maximum, jnp.max(scores, axis=-1))
    factor = jnp.exp(row_maximum - new_max)
    weights = jnp.exp(scores - new_max[..., None])
    row_total = row_total * factor + jnp.sum(weights, axis=-1)
    weighted = weighted * factor[..., None] + jnp.einsum(
        "ihj,jhe->ihe",
        weights.astype(jnp.bfloat16),
        value_entries,
        preferred_element_type=jnp.float32,
    )
    return (new_max, row_total, weighted)


def local_block(queries, key_vectors, values, directions, beta_logit, sub_size):
    row_count, head_count, head_width = queries.shape
    score_scale = head_width ** (-0.5)
    unit_dirs = unit_rows(directions)
    beta_rate = 2.0 / (1.0 + jnp.exp(-beta_logit.astype(jnp.float32)))
    inner_scores, start_query, end_keys, transport = sub_blocks(
        queries.astype(jnp.float32), key_vectors.astype(jnp.float32), unit_dirs, beta_rate, sub_size
    )
    combined_parts, framed_query_rows, frame_keys, frame_map = frames(
        inner_scores, start_query, end_keys, transport, sub_size, score_scale
    )
    frame_count = combined_parts.shape[0]
    frame_size = 2 * sub_size
    frame_values = values.reshape(frame_count, frame_size, head_count, head_width)
    softmax_state = start_state(combined_parts, frame_values)
    frame_half = frame_keys.astype(jnp.bfloat16)
    frame_of_row = lax.iota(jnp.int32, row_count) // frame_size
    identity_heads = jnp.broadcast_to(
        jnp.eye(head_width, dtype=jnp.float32), (head_count, head_width, head_width)
    )

    def descend(running, block_index):
        current, softmax_state = running
        is_later = (frame_of_row > block_index)[:, None, None]
        scores = (
            jnp.einsum(
                "ihe,jhe->ihj",
                current.astype(jnp.bfloat16),
                frame_half[block_index],
                preferred_element_type=jnp.float32,
            )
            * score_scale
        )
        scores = jnp.where(is_later, scores, far_below)
        softmax_state = absorb(softmax_state, scores, frame_values[block_index])
        advanced = jnp.einsum("ihe,hek->ihk", current, frame_map[block_index], precision=precise)
        return ((jnp.where(is_later, advanced, current), softmax_state), None)

    (block_query, softmax_state), _ = lax.scan(
        descend,
        (framed_query_rows.reshape(row_count, head_count, head_width), softmax_state),
        jnp.arange(frame_count - 1, -1, -1, dtype=jnp.int32),
    )

    def ascend(running, block_index):
        current, product = running
        is_earlier = (frame_of_row < block_index)[:, None, None]
        advanced = jnp.einsum("jhk,hek->jhe", current, frame_map[block_index], precision=precise)
        product = jnp.einsum("hek,hkg->heg", frame_map[block_index], product, precision=precise)
        return ((jnp.where(is_earlier, advanced, current), product), None)

    (block_keys, block_map), _ = lax.scan(
        ascend,
        (frame_keys.reshape(row_count, head_count, head_width), identity_heads),
        jnp.arange(frame_count, dtype=jnp.int32),
    )
    return (softmax_state, block_query, block_keys.astype(jnp.bfloat16), block_map)


def remote_absorb(
    softmax_state, block_query, carried_map, key_half, value_entries, is_valid, score_scale
):
    moved_query = jnp.einsum("ihe,hek->ihk", block_query, carried_map, precision=precise).astype(
        jnp.bfloat16
    )
    scores = (
        jnp.einsum("ihe,jhe->ihj", moved_query, key_half, preferred_element_type=jnp.float32)
        * score_scale
    )
    scores = jnp.where(is_valid, scores, far_below)
    return absorb(softmax_state, scores, value_entries)


def shards(queries, key_vectors, values, directions, beta_logit):
    groups = lax.axis_size("head")
    local_rows, head_total, head_width = queries.shape
    split_heads = (local_rows, groups, head_total // groups, head_width)
    grouped = (
        queries.reshape(split_heads),
        key_vectors.reshape(split_heads),
        values.reshape(split_heads),
        directions.reshape(split_heads),
        beta_logit.reshape(split_heads[:3]),
    )
    pieces = (
        lax.all_to_all(grouped[0], "head", split_axis=1, concat_axis=0, tiled=True),
        lax.all_to_all(grouped[1], "head", split_axis=1, concat_axis=0, tiled=True),
        lax.all_to_all(grouped[2], "head", split_axis=1, concat_axis=0, tiled=True),
        lax.all_to_all(grouped[3], "head", split_axis=1, concat_axis=0, tiled=True),
        lax.all_to_all(grouped[4], "head", split_axis=1, concat_axis=0, tiled=True),
    )
    head_query, head_keys, value_entries, head_dirs, head_logit = [
        piece_array[:, 0] for piece_array in pieces
    ]
    row_count, head_count, attend_head_width = head_query.shape
    score_scale = attend_head_width ** (-0.5)
    softmax_state, block_query, block_keys, block_map = local_block(
        head_query, head_keys, value_entries, head_dirs, head_logit, SUB
    )
    own_block = lax.axis_index("ctx")
    sections = lax.axis_size("ctx")
    identity_heads = jnp.broadcast_to(
        jnp.eye(attend_head_width, dtype=jnp.float32),
        (head_count, attend_head_width, attend_head_width),
    )

    def relay_hop(hop_index, running):
        moving_keys, moving_values, moving_map, inner_state = running
        moving_keys, moving_values = from_behind((moving_keys, moving_values), "ctx", 1)
        moving_map = from_behind(moving_map, "ctx", 1)
        inner_state = remote_absorb(
            inner_state,
            block_query,
            moving_map,
            moving_keys,
            moving_values,
            own_block >= hop_index,
            score_scale,
        )
        moving_map = jnp.einsum("hek,hkg->heg", block_map, moving_map, precision=precise)
        return (moving_keys, moving_values, moving_map, inner_state)

    running = lax.fori_loop(
        1, sections, relay_hop, (block_keys, value_entries, identity_heads, softmax_state)
    )
    softmax_state = running[3]
    row_maximum, row_total, weighted = softmax_state
    per_head = (weighted / row_total[..., None]).astype(jnp.bfloat16)[:, None]
    returned = lax.all_to_all(per_head, "head", split_axis=0, concat_axis=1, tiled=True)
    return returned.reshape(local_rows, head_total, head_width)


def solution(mesh):
    in_specs = (
        P(("ctx", "head"), None, None),
        P(("ctx", "head"), None, None),
        P(("ctx", "head"), None, None),
        P(("ctx", "head"), None, None),
        P(("ctx", "head"), None),
    )
    out_specs = P(("ctx", "head"), None, None)
    return jax.shard_map(shards, mesh=mesh, in_specs=in_specs, out_specs=out_specs, check_vma=False)
```

profile of v0, /device:TPU:26, one launch (start us, length us, event | category | flops | bytes accessed | tf_op | source)
XLA Modules:
  0.0 637.3 jit_solution(12609533034290747592)
XLA Ops:
  0.0 4.2 all-to-all-start.1
  7.5 4.9 all-to-all-start
  15.7 5.8 all-to-all-done
  21.5 4.7 all-to-all-start.4
  27.5 2.6 select_bitcast_fusion
  30.2 236.6 %custom-call.4 = f32[6,8,1,64,64]{3,4,2,1,0:T(8,128)} custom-call(f32[6,8,1,64,64]{4,3,2,1,0:T(8,128)S(1)} %select_bitcast_fusion), custom_call_target="InvertDiagBlocksLowerTriangular" | custom-call | tf_op jit(solution)/shard_map/jit(_solve_triangular)/vmap(vmap())/triangular_solve | solution.py:38
  266.8 4.0 fusion.49
  270.9 4.4 all-to-all-start.2
  275.3 2.6 fusion.59
  280.9 4.1 bitcast_subtract_fusion.2
  285.1 5.1 all-to-all-start.3
  290.3 2.6 bitcast_select_fusion.4
  292.9 2.6 fusion.87
  295.5 2.6 fusion.88
  298.2 2.7 fusion.65
  300.9 3.1 bitcast_subtract_fusion.3
  305.6 5.2 convolution_subtract_fusion
  313.3 3.1 fusion.58
  323.1 2.9 fusion.52
  332.1 39.8 %while.55 = (s32[]{:T(128)}, f32[384,8,128]{0,2,1:T(8,128)S(1)}, f32[384,8]{0,1:T(8,128)S(1)}, f32[384,8]{0,1:T(8,128)S(1)}, f32[384,8,128]{0,2,1:T(8,128)}, /*i...) while((s32[]{:T(128)}, f32[384,8,128]{0,2,1:T(8,128)S(1)}, ...), condition=%wide.region_8.9_spmd.clone, body=%wide.region_5.8_spmd.clone.sunk | while | flops 809641344 | bytes 19596724 | solution.py:158
  339.9 3.0 bitcast_add_fusion.5
  342.8 2.6 bitcast_select_fusion.8
  353.1 3.0 bitcast_add_fusion.5
  356.1 2.6 bitcast_select_fusion.8
  366.4 3.0 bitcast_add_fusion.5
  375.5 3.5 copy.207
  381.7 23.3 %while.54 = (s32[]{:T(128)}, f32[384,8,128]{0,2,1:T(8,128)S(1)}, f32[8,128,128]{2,1,0:T(8,128)}, s32[3]{0:T(128)S(1)}, f32[3,8,128,128]{3,2,1,0:T(8,128)}, /*index=5*/s32[]{:T(128)}, s32[]{:T(128)}, s32[]{:T(128)}) while((s32[]{:T(128)}, f32[384,8,128]{0,2,1:T(8,128)S(1)}, f32[8,128,128]{2,1,0:T(8,128)}, s32[3]{0:T(128)S(1)}, ...), condition=%wide.region_2.3_spmd.clone, body=%wide.region_1.2_spmd.clone.sunk | while | flops 805703040 | bytes 19399752 | solution.py:171
  411.2 212.1 %while.53 = (s32[]{:T(128)}, bf16[384,8,128]{2,0,1:T(8,128)(2,1)}, bf16[384,8,128]{2,0,1:T(8,128)(2,1)}, f32[8,128,128]{2,1,0:T(8,128)}, f32[384,8]{0,1:T(8,128)...) while((s32[]{:T(128)}, bf16[384,8,128]{2,0,1:T(8,128)(2,1)}, ...), condition=%wide.region_12.13_spmd, body=%wide.region_9.12_spmd.sunk | while | flops 1423448064 | bytes 42139912 | solution.py:242
  417.0 5.0 collective-permute-done.2
  422.0 2.6 fusion.139
  424.6 2.9 fusion.140
  427.5 2.8 collective-permute-done
  433.0 5.7 collective-permute-done.1
  447.3 5.0 collective-permute-done.2
  452.3 2.6 fusion.139
  454.9 2.9 fusion.140
  457.8 2.8 collective-permute-done
  463.3 5.7 collective-permute-done.1
  477.6 5.0 collective-permute-done.2
  482.6 2.6 fusion.139
  485.2 2.9 fusion.140
  488.1 2.8 collective-permute-done
  493.6 5.7 collective-permute-done.1
  507.9 5.0 collective-permute-done.2
  512.9 2.6 fusion.139
  515.5 2.9 fusion.140
  518.4 2.8 collective-permute-done
  523.9 5.7 collective-permute-done.1
  538.2 5.0 collective-permute-done.2
  543.2 2.6 fusion.139
  545.8 2.9 fusion.140
  548.7 2.8 collective-permute-done
  554.2 5.7 collective-permute-done.1
  568.5 5.0 collective-permute-done.2
  573.5 2.6 fusion.139
  576.1 2.9 fusion.140
  579.0 2.8 collective-permute-done
  584.5 5.7 collective-permute-done.1
  598.8 5.0 collective-permute-done.2
  603.8 2.6 fusion.139
  606.4 2.9 fusion.140
  609.3 2.8 collective-permute-done
  614.8 5.7 collective-permute-done.1
  624.4 11.4 %all_to_all.78 = bf16[384,1,8,128]{3,2,1,0:T(8,128)(2,1)S(1)} all-to-all(bf16[384,1,8,128]{3,2,1,0:T(8,128)(2,1)S(1)} %fusion.73), channel_id=1, replica_groups=mesh['ctx'=8,'head'=4] {'head'}, dimensions={0} | all-to-all | bytes 1572864 | tf_op jit(solution)/shard_map/all_to_all | solution.py:248
  (219 shorter events, 157.1 us)
Async XLA Ops:
  0.0 7.5 %all-to-all-start.1 = ((bf16[96,4,8]{0,2,1:T(8,128)(2,1)}), bf16[96,4,8]{0,2,1:T(8,128)(2,1)S(1)}, u32[]{:S(2)}, u32[]{:S(2)}) async-start(bf16[96,4,8]{0,2,1:T(8,128)(2,1)} %bitcast.273), calls=%async_computation.1 | async-start | bytes 16384 | tf_op jit(solution)/shard_map/all_to_all | solution.py:209
  4.3 8.1 %copy-start.7 = (bf16[96,32,128]{2,1,0:T(8,128)(2,1)S(1)}, bf16[96,32,128]{2,1,0:T(8,128)(2,1)}, u32[]{:S(2)}) copy-start(bf16[96,32,128]{2,1,0:T(8,128)(2,1)} %param.11) | copy-start | bytes 2359300
  6.5 7.0 %copy-start.8 = (bf16[96,32,128]{2,1,0:T(8,128)(2,1)S(1)}, bf16[96,32,128]{2,1,0:T(8,128)(2,1)}, u32[]{:S(2)}) copy-start(bf16[96,32,128]{2,1,0:T(8,128)(2,1)} %param.12) | copy-start | bytes 2359300
  7.5 14.0 %all-to-all-start = ((bf16[96,4,8,128]{3,2,0,1:T(8,128)(2,1)}), bf16[96,4,8,128]{3,2,0,1:T(8,128)(2,1)S(1)}, u32[]{:S(2)}, u32[]{:S(2)}) async-start(bf16[96,4,8,128]{3,2,0,1:T(8,128)(2,1)} %copy.186), calls=%async_computation | async-start | bytes 1572864 | tf_op jit(solution)/shard_map/all_to_all | solution.py:208
  12.4 2.1 copy-start.9
  21.5 249.4 %all-to-all-start.4 = ((bf16[96,4,8,128]{3,2,0,1:T(8,128)(2,1)}), bf16[96,4,8,128]{3,2,0,1:T(8,128)(2,1)}, u32[]{:S(2)}, u32[]{:S(2)}) async-start(bf16[96,4,8,128]{3,2,0,1:T(8,128)(2,1)} %copy.211), calls=%async_computation.4 | async-start | bytes 1572864 | tf_op jit(solution)/shard_map/all_to_all | solution.py:205
  270.9 14.3 %all-to-all-start.2 = ((bf16[96,4,8,128]{3,2,0,1:T(8,128)(2,1)}), bf16[96,4,8,128]{3,2,0,1:T(8,128)(2,1)}, u32[]{:S(2)}, u32[]{:S(2)}) async-start(bf16[96,4,8,128]{3,2,0,1:T(8,128)(2,1)} %copy.199), calls=%async_computation.2 | async-start | bytes 1572864 | tf_op jit(solution)/shard_map/all_to_all | solution.py:206
  279.7 1.2 copy-start.3
  285.1 40.8 %all-to-all-start.3 = ((bf16[96,4,8,128]{3,2,0,1:T(8,128)(2,1)}), bf16[96,4,8,128]{3,2,0,1:T(8,128)(2,1)}, u32[]{:S(2)}, u32[]{:S(2)}) async-start(bf16[96,4,8,128]{3,2,0,1:T(8,128)(2,1)} %copy.210), calls=%async_computation.3 | async-start | bytes 1572864 | tf_op jit(solution)/shard_map/all_to_all | solution.py:207
  292.8 2.7 copy-start.4
  300.9 3.1 copy-start.5
  328.8 1.7 copy-start.6
  385.1 1.4 copy-start.2
  386.5 1.5 copy-start
  392.8 1.4 copy-start.2
  394.2 1.5 copy-start
  400.5 1.4 copy-start.2
  401.9 1.5 copy-start
  411.2 10.8 %collective-permute-start.2 = (f32[8,128,128]{2,1,0:T(8,128)}, f32[8,128,128]{2,1,0:T(8,128)}, u32[]{:S(2)}, u32[]{:S(2)}) collective-permute-start(f32[8,128,128]{2,1,0:T(8,128)} %get-tuple-element.715), channel_id=1, source_target_pairs={{0,4},{4,8},{8,12},{12,16},{16,20},{20,24},{24,28},{1,5},{5,9},{9,... | collective-permute-start | bytes 1572872 | tf_op jit(solution)/shard_map/while/body/eval_jaxpr/ppermute | solution.py:16
  413.1 17.2 %collective-permute-start = (bf16[384,8,128]{2,0,1:T(8,128)(2,1)}, bf16[384,8,128]{2,0,1:T(8,128)(2,1)S(1)}, u32[]{:S(2)}, u32[]{:S(2)}) collective-permute-start(bf16[384,8,128]{2,0,1:T(8,128)(2,1)} %get-tuple-element.713), channel_id=1, source_target_pairs={{0,4},{4,8},{8,12},{12,16},{16,20},{20,24},{24,28},{1,5},{5,9},{9,... | collective-permute-start | bytes 2359304 | tf_op jit(solution)/shard_map/while/body/eval_jaxpr/ppermute | solution.py:16
  415.0 23.7 %collective-permute-start.1 = (bf16[384,8,128]{2,0,1:T(8,128)(2,1)}, bf16[384,8,128]{2,0,1:T(8,128)(2,1)S(1)}, u32[]{:S(2)}, u32[]{:S(2)}) collective-permute-start(bf16[384,8,128]{2,0,1:T(8,128)(2,1)} %get-tuple-element.714), channel_id=1, source_target_pairs={{0,4},{4,8},{8,12},{12,16},{16,20},{20,24},{24,28},{1,5},{5,9},{9,... | collective-permute-start | bytes 2359304 | tf_op jit(solution)/shard_map/while/body/eval_jaxpr/ppermute | solution.py:16
  417.0 7.7 %copy-start.1 = (f32[384,8,128]{2,0,1:T(8,128)S(1)}, f32[384,8,128]{2,0,1:T(8,128)}, u32[]{:S(2)}) copy-start(f32[384,8,128]{2,0,1:T(8,128)} %get-tuple-element.732) | copy-start | bytes 4718596 | tf_op jit(solution)/shard_map/while
  441.5 10.8 %collective-permute-start.2 = (f32[8,128,128]{2,1,0:T(8,128)}, f32[8,128,128]{2,1,0:T(8,128)}, u32[]{:S(2)}, u32[]{:S(2)}) collective-permute-start(f32[8,128,128]{2,1,0:T(8,128)} %get-tuple-element.715), channel_id=1, source_target_pairs={{0,4},{4,8},{8,12},{12,16},{16,20},{20,24},{24,28},{1,5},{5,9},{9,... | collective-permute-start | bytes 1572872 | tf_op jit(solution)/shard_map/while/body/eval_jaxpr/ppermute | solution.py:16
  443.4 17.2 %collective-permute-start = (bf16[384,8,128]{2,0,1:T(8,128)(2,1)}, bf16[384,8,128]{2,0,1:T(8,128)(2,1)S(1)}, u32[]{:S(2)}, u32[]{:S(2)}) collective-permute-start(bf16[384,8,128]{2,0,1:T(8,128)(2,1)} %get-tuple-element.713), channel_id=1, source_target_pairs={{0,4},{4,8},{8,12},{12,16},{16,20},{20,24},{24,28},{1,5},{5,9},{9,... | collective-permute-start | bytes 2359304 | tf_op jit(solution)/shard_map/while/body/eval_jaxpr/ppermute | solution.py:16
  445.3 23.7 %collective-permute-start.1 = (bf16[384,8,128]{2,0,1:T(8,128)(2,1)}, bf16[384,8,128]{2,0,1:T(8,128)(2,1)S(1)}, u32[]{:S(2)}, u32[]{:S(2)}) collective-permute-start(bf16[384,8,128]{2,0,1:T(8,128)(2,1)} %get-tuple-element.714), channel_id=1, source_target_pairs={{0,4},{4,8},{8,12},{12,16},{16,20},{20,24},{24,28},{1,5},{5,9},{9,... | collective-permute-start | bytes 2359304 | tf_op jit(solution)/shard_map/while/body/eval_jaxpr/ppermute | solution.py:16
  447.3 7.7 %copy-start.1 = (f32[384,8,128]{2,0,1:T(8,128)S(1)}, f32[384,8,128]{2,0,1:T(8,128)}, u32[]{:S(2)}) copy-start(f32[384,8,128]{2,0,1:T(8,128)} %get-tuple-element.732) | copy-start | bytes 4718596 | tf_op jit(solution)/shard_map/while
  471.8 10.8 %collective-permute-start.2 = (f32[8,128,128]{2,1,0:T(8,128)}, f32[8,128,128]{2,1,0:T(8,128)}, u32[]{:S(2)}, u32[]{:S(2)}) collective-permute-start(f32[8,128,128]{2,1,0:T(8,128)} %get-tuple-element.715), channel_id=1, source_target_pairs={{0,4},{4,8},{8,12},{12,16},{16,20},{20,24},{24,28},{1,5},{5,9},{9,... | collective-permute-start | bytes 1572872 | tf_op jit(solution)/shard_map/while/body/eval_jaxpr/ppermute | solution.py:16
  473.7 17.2 %collective-permute-start = (bf16[384,8,128]{2,0,1:T(8,128)(2,1)}, bf16[384,8,128]{2,0,1:T(8,128)(2,1)S(1)}, u32[]{:S(2)}, u32[]{:S(2)}) collective-permute-start(bf16[384,8,128]{2,0,1:T(8,128)(2,1)} %get-tuple-element.713), channel_id=1, source_target_pairs={{0,4},{4,8},{8,12},{12,16},{16,20},{20,24},{24,28},{1,5},{5,9},{9,... | collective-permute-start | bytes 2359304 | tf_op jit(solution)/shard_map/while/body/eval_jaxpr/ppermute | solution.py:16
  475.6 23.7 %collective-permute-start.1 = (bf16[384,8,128]{2,0,1:T(8,128)(2,1)}, bf16[384,8,128]{2,0,1:T(8,128)(2,1)S(1)}, u32[]{:S(2)}, u32[]{:S(2)}) collective-permute-start(bf16[384,8,128]{2,0,1:T(8,128)(2,1)} %get-tuple-element.714), channel_id=1, source_target_pairs={{0,4},{4,8},{8,12},{12,16},{16,20},{20,24},{24,28},{1,5},{5,9},{9,... | collective-permute-start | bytes 2359304 | tf_op jit(solution)/shard_map/while/body/eval_jaxpr/ppermute | solution.py:16
  477.6 7.7 %copy-start.1 = (f32[384,8,128]{2,0,1:T(8,128)S(1)}, f32[384,8,128]{2,0,1:T(8,128)}, u32[]{:S(2)}) copy-start(f32[384,8,128]{2,0,1:T(8,128)} %get-tuple-element.732) | copy-start | bytes 4718596 | tf_op jit(solution)/shard_map/while
  502.1 10.8 %collective-permute-start.2 = (f32[8,128,128]{2,1,0:T(8,128)}, f32[8,128,128]{2,1,0:T(8,128)}, u32[]{:S(2)}, u32[]{:S(2)}) collective-permute-start(f32[8,128,128]{2,1,0:T(8,128)} %get-tuple-element.715), channel_id=1, source_target_pairs={{0,4},{4,8},{8,12},{12,16},{16,20},{20,24},{24,28},{1,5},{5,9},{9,... | collective-permute-start | bytes 1572872 | tf_op jit(solution)/shard_map/while/body/eval_jaxpr/ppermute | solution.py:16
  504.0 17.2 %collective-permute-start = (bf16[384,8,128]{2,0,1:T(8,128)(2,1)}, bf16[384,8,128]{2,0,1:T(8,128)(2,1)S(1)}, u32[]{:S(2)}, u32[]{:S(2)}) collective-permute-start(bf16[384,8,128]{2,0,1:T(8,128)(2,1)} %get-tuple-element.713), channel_id=1, source_target_pairs={{0,4},{4,8},{8,12},{12,16},{16,20},{20,24},{24,28},{1,5},{5,9},{9,... | collective-permute-start | bytes 2359304 | tf_op jit(solution)/shard_map/while/body/eval_jaxpr/ppermute | solution.py:16
  505.9 23.7 %collective-permute-start.1 = (bf16[384,8,128]{2,0,1:T(8,128)(2,1)}, bf16[384,8,128]{2,0,1:T(8,128)(2,1)S(1)}, u32[]{:S(2)}, u32[]{:S(2)}) collective-permute-start(bf16[384,8,128]{2,0,1:T(8,128)(2,1)} %get-tuple-element.714), channel_id=1, source_target_pairs={{0,4},{4,8},{8,12},{12,16},{16,20},{20,24},{24,28},{1,5},{5,9},{9,... | collective-permute-start | bytes 2359304 | tf_op jit(solution)/shard_map/while/body/eval_jaxpr/ppermute | solution.py:16
  507.9 7.7 %copy-start.1 = (f32[384,8,128]{2,0,1:T(8,128)S(1)}, f32[384,8,128]{2,0,1:T(8,128)}, u32[]{:S(2)}) copy-start(f32[384,8,128]{2,0,1:T(8,128)} %get-tuple-element.732) | copy-start | bytes 4718596 | tf_op jit(solution)/shard_map/while
  532.4 10.8 %collective-permute-start.2 = (f32[8,128,128]{2,1,0:T(8,128)}, f32[8,128,128]{2,1,0:T(8,128)}, u32[]{:S(2)}, u32[]{:S(2)}) collective-permute-start(f32[8,128,128]{2,1,0:T(8,128)} %get-tuple-element.715), channel_id=1, source_target_pairs={{0,4},{4,8},{8,12},{12,16},{16,20},{20,24},{24,28},{1,5},{5,9},{9,... | collective-permute-start | bytes 1572872 | tf_op jit(solution)/shard_map/while/body/eval_jaxpr/ppermute | solution.py:16
  534.3 17.2 %collective-permute-start = (bf16[384,8,128]{2,0,1:T(8,128)(2,1)}, bf16[384,8,128]{2,0,1:T(8,128)(2,1)S(1)}, u32[]{:S(2)}, u32[]{:S(2)}) collective-permute-start(bf16[384,8,128]{2,0,1:T(8,128)(2,1)} %get-tuple-element.713), channel_id=1, source_target_pairs={{0,4},{4,8},{8,12},{12,16},{16,20},{20,24},{24,28},{1,5},{5,9},{9,... | collective-permute-start | bytes 2359304 | tf_op jit(solution)/shard_map/while/body/eval_jaxpr/ppermute | solution.py:16
  536.2 23.7 %collective-permute-start.1 = (bf16[384,8,128]{2,0,1:T(8,128)(2,1)}, bf16[384,8,128]{2,0,1:T(8,128)(2,1)S(1)}, u32[]{:S(2)}, u32[]{:S(2)}) collective-permute-start(bf16[384,8,128]{2,0,1:T(8,128)(2,1)} %get-tuple-element.714), channel_id=1, source_target_pairs={{0,4},{4,8},{8,12},{12,16},{16,20},{20,24},{24,28},{1,5},{5,9},{9,... | collective-permute-start | bytes 2359304 | tf_op jit(solution)/shard_map/while/body/eval_jaxpr/ppermute | solution.py:16
  538.1 7.7 %copy-start.1 = (f32[384,8,128]{2,0,1:T(8,128)S(1)}, f32[384,8,128]{2,0,1:T(8,128)}, u32[]{:S(2)}) copy-start(f32[384,8,128]{2,0,1:T(8,128)} %get-tuple-element.732) | copy-start | bytes 4718596 | tf_op jit(solution)/shard_map/while
  562.7 10.8 %collective-permute-start.2 = (f32[8,128,128]{2,1,0:T(8,128)}, f32[8,128,128]{2,1,0:T(8,128)}, u32[]{:S(2)}, u32[]{:S(2)}) collective-permute-start(f32[8,128,128]{2,1,0:T(8,128)} %get-tuple-element.715), channel_id=1, source_target_pairs={{0,4},{4,8},{8,12},{12,16},{16,20},{20,24},{24,28},{1,5},{5,9},{9,... | collective-permute-start | bytes 1572872 | tf_op jit(solution)/shard_map/while/body/eval_jaxpr/ppermute | solution.py:16
  564.6 17.2 %collective-permute-start = (bf16[384,8,128]{2,0,1:T(8,128)(2,1)}, bf16[384,8,128]{2,0,1:T(8,128)(2,1)S(1)}, u32[]{:S(2)}, u32[]{:S(2)}) collective-permute-start(bf16[384,8,128]{2,0,1:T(8,128)(2,1)} %get-tuple-element.713), channel_id=1, source_target_pairs={{0,4},{4,8},{8,12},{12,16},{16,20},{20,24},{24,28},{1,5},{5,9},{9,... | collective-permute-start | bytes 2359304 | tf_op jit(solution)/shard_map/while/body/eval_jaxpr/ppermute | solution.py:16
  566.5 23.7 %collective-permute-start.1 = (bf16[384,8,128]{2,0,1:T(8,128)(2,1)}, bf16[384,8,128]{2,0,1:T(8,128)(2,1)S(1)}, u32[]{:S(2)}, u32[]{:S(2)}) collective-permute-start(bf16[384,8,128]{2,0,1:T(8,128)(2,1)} %get-tuple-element.714), channel_id=1, source_target_pairs={{0,4},{4,8},{8,12},{12,16},{16,20},{20,24},{24,28},{1,5},{5,9},{9,... | collective-permute-start | bytes 2359304 | tf_op jit(solution)/shard_map/while/body/eval_jaxpr/ppermute | solution.py:16
  568.4 7.7 %copy-start.1 = (f32[384,8,128]{2,0,1:T(8,128)S(1)}, f32[384,8,128]{2,0,1:T(8,128)}, u32[]{:S(2)}) copy-start(f32[384,8,128]{2,0,1:T(8,128)} %get-tuple-element.732) | copy-start | bytes 4718596 | tf_op jit(solution)/shard_map/while
  593.0 10.8 %collective-permute-start.2 = (f32[8,128,128]{2,1,0:T(8,128)}, f32[8,128,128]{2,1,0:T(8,128)}, u32[]{:S(2)}, u32[]{:S(2)}) collective-permute-start(f32[8,128,128]{2,1,0:T(8,128)} %get-tuple-element.715), channel_id=1, source_target_pairs={{0,4},{4,8},{8,12},{12,16},{16,20},{20,24},{24,28},{1,5},{5,9},{9,... | collective-permute-start | bytes 1572872 | tf_op jit(solution)/shard_map/while/body/eval_jaxpr/ppermute | solution.py:16
  594.9 17.2 %collective-permute-start = (bf16[384,8,128]{2,0,1:T(8,128)(2,1)}, bf16[384,8,128]{2,0,1:T(8,128)(2,1)S(1)}, u32[]{:S(2)}, u32[]{:S(2)}) collective-permute-start(bf16[384,8,128]{2,0,1:T(8,128)(2,1)} %get-tuple-element.713), channel_id=1, source_target_pairs={{0,4},{4,8},{8,12},{12,16},{16,20},{20,24},{24,28},{1,5},{5,9},{9,... | collective-permute-start | bytes 2359304 | tf_op jit(solution)/shard_map/while/body/eval_jaxpr/ppermute | solution.py:16
  596.8 23.7 %collective-permute-start.1 = (bf16[384,8,128]{2,0,1:T(8,128)(2,1)}, bf16[384,8,128]{2,0,1:T(8,128)(2,1)S(1)}, u32[]{:S(2)}, u32[]{:S(2)}) collective-permute-start(bf16[384,8,128]{2,0,1:T(8,128)(2,1)} %get-tuple-element.714), channel_id=1, source_target_pairs={{0,4},{4,8},{8,12},{12,16},{16,20},{20,24},{24,28},{1,5},{5,9},{9,... | collective-permute-start | bytes 2359304 | tf_op jit(solution)/shard_map/while/body/eval_jaxpr/ppermute | solution.py:16
  598.7 7.7 %copy-start.1 = (f32[384,8,128]{2,0,1:T(8,128)S(1)}, f32[384,8,128]{2,0,1:T(8,128)}, u32[]{:S(2)}) copy-start(f32[384,8,128]{2,0,1:T(8,128)} %get-tuple-element.732) | copy-start | bytes 4718596 | tf_op jit(solution)/shard_map/while
where the time goes:
time: 649 us; the launch traced here: 637 us
  other arithmetic  256 us (39%)
  matrix products  135 us (21%)
  waiting for transfers between devices  102 us (16%)
  starting transfers between devices  63.8 us (10%)
  local copies, waits for them, and re-layouts  56.2 us (9%)
  loops' own time  13 us (2%)
  blocking collectives  11.4 us (2%)
    another operation x2, other arithmetic, sub_blocks(): jax.scipy.linalg.solve_triangular(triangle, jnp.broadcast_to(identity_sub...  237 us
    ppermute x21, waiting for transfers between devices, from_behind(): return lax.ppermute(value, axis, pairs)  94.6 us
    ppermute x21, starting transfers between devices, from_behind(): return lax.ppermute(value, axis, pairs)  40.3 us
    dot_general x10, matrix products, absorb(): jnp.einsum('ihj,jhe->ihe', weights.astype(jnp.bfloat16), value_entries, p...  21.7 us
    dot_general x7, matrix products, remote_absorb(): jnp.einsum('ihe,hek->ihk', block_query, carried_map, precision=precise)  20.4 us
    dot_general x7, matrix products, relay_hop(): jnp.einsum('hek,hkg->heg', block_map, moving_map, precision=precise)  18.4 us
    while x59, local copies, waits for them, and re-layouts  17 us
  transfers between devices with their start and end apart: 26, of which 24 were waited for; matrix products, arithmetic and copies ran while one was open for 55% of the time, Pallas kernels for 0%

commit v1 on v0

v1 whole, which is shorter than its diff:
```python
import functools

import jax
import jax.numpy as jnp
from jax import lax
from jax.experimental import pallas as pl
from jax.experimental.pallas import tpu as pltpu
from jax.sharding import PartitionSpec as P

SUB = 64
f32 = jnp.float32
bf16 = jnp.bfloat16
far_below = -1e30


def split_two(a):
    high = a.astype(bf16)
    return high, (a - high.astype(f32)).astype(bf16)


def mm(a, b):
    return lax.dot_general(a, b, (((1,), (0,)), ((), ())), preferred_element_type=f32)


def mm_nt(a, b):
    return lax.dot_general(a, b, (((1,), (1,)), ((), ())), preferred_element_type=f32)


def wide(a, b):
    n = b.shape[1]
    ah, al = split_two(a)
    bh, bl = split_two(b)
    row = jnp.concatenate([bh, bl], axis=1)
    out = mm(jnp.concatenate([ah, al], axis=1), jnp.concatenate([row, row], axis=0))
    return out[:, :n] + out[:, n:]


def wide_nt(a, b):
    n = b.shape[0]
    ah, al = split_two(a)
    bh, bl = split_two(b)
    col = jnp.concatenate([bh, bl], axis=0)
    out = mm_nt(jnp.concatenate([ah, al], axis=1), jnp.concatenate([col, col], axis=1))
    return out[:, :n] + out[:, n:]


def half_wide(a, b_half):
    ah, al = split_two(a)
    return mm(jnp.concatenate([ah, al], axis=1), jnp.concatenate([b_half, b_half], axis=0))


def local_head(q_all, k_all, v_all, d_all, logit_row, frame):
    rows, width = q_all.shape
    count = rows // frame
    scale = width ** (-0.5)
    row_at = lax.broadcasted_iota(jnp.int32, (frame, frame), 0)
    col_at = lax.broadcasted_iota(jnp.int32, (frame, frame), 1)
    diagonal = row_at == col_at
    below = row_at > col_at
    eye = jnp.where(diagonal, 1.0, 0.0).astype(f32)

    def to_row(col):
        return jnp.sum(jnp.where(diagonal, col, 0.0), axis=0, keepdims=True)

    def to_col(row):
        return jnp.sum(jnp.where(diagonal, row, 0.0), axis=1, keepdims=True)

    rate_row = 2.0 / (1.0 + jnp.exp(-logit_row))
    q, k, v, d, strict, inverse, left, right = [], [], [], [], [], [], [], []
    for f in range(count):
        at = slice(f * frame, (f + 1) * frame)
        qf, kf, vf, df = [x[at].astype(bf16) for x in (q_all, k_all, v_all, d_all)]
        d32 = d_all[at]
        s = lax.rsqrt(jnp.sum(d32 * d32, axis=1, keepdims=True) + 1e-06)
        s_row = to_row(s)
        rate = rate_row[:, at]
        gram = mm_nt(df, df)
        near = jnp.where(below, gram * (to_col(rate) * s) * s_row, 0.0)
        q.append(qf), k.append(kf), v.append(vf), d.append(df)
        strict.append(near), left.append(s), right.append(rate * s_row)
        inverse.append(eye - jnp.where((row_at // 2) == (col_at // 2), near, 0.0))
    size = 2
    while size < frame:
        corner = ((row_at // (2 * size)) == (col_at // (2 * size))) & (
            (row_at // size) != (col_at // size)
        )
        step = [wide(jnp.where(corner, strict[f], 0.0), inverse[f]) for f in range(count)]
        inverse = [inverse[f] - wide(inverse[f], step[f]) for f in range(count)]
        size *= 2
    inner, query, keys, maps = [], [], [], []
    for f in range(count):
        y = inverse[f] * left[f] * right[f]
        query_dots = jnp.where(row_at >= col_at, mm_nt(q[f], d[f]), 0.0)
        key_dots = jnp.where(row_at < col_at, mm_nt(k[f], d[f]), 0.0)
        query_mix = wide(query_dots, y)
        key_mix = wide_nt(key_dots, y)
        scores = mm_nt(q[f], k[f]) - wide_nt(query_mix, key_dots)
        inner.append(jnp.where(row_at >= col_at, scores * scale, far_below))
        query.append(q[f].astype(f32) - half_wide(query_mix, d[f]))
        keys.append(k[f].astype(f32) - half_wide(key_mix, d[f]))
        pushed = half_wide(y, d[f])
        ph, plow = split_two(pushed)
        both = mm(d[f].T, jnp.concatenate([ph, plow], axis=1))
        maps.append(eye - (both[:, :width] + both[:, width:]))
    half = [x.astype(bf16) for x in keys]
    maxima, totals, sums, block_query, block_keys = [], [], [], [], []
    for f in range(count):
        current = query[f]
        parts = [inner[f]]
        vals = [v[f]]
        for g in range(f - 1, -1, -1):
            parts.append(mm_nt(current.astype(bf16), half[g]) * scale)
            vals.append(v[g])
            current = wide(current, maps[g])
        block_query.append(current)
        top = parts[0]
        for p in parts[1:]:
            top = jnp.maximum(top, p)
        top = jnp.max(top, axis=1, keepdims=True)
        total = 0.0
        weighted = 0.0
        for p, vv in zip(parts, vals):
            w = jnp.exp(p - top)
            total = total + jnp.sum(w, axis=1, keepdims=True)
            weighted = weighted + mm(w.astype(bf16), vv)
        maxima.append(top), totals.append(total), sums.append(weighted)
    product = maps[0]
    for f in range(1, count):
        product = wide(maps[f], product)
    for g in range(count):
        moved = keys[g]
        for f in range(g + 1, count):
            moved = wide_nt(moved, maps[f])
        block_keys.append(moved)
    cat = lambda xs: jnp.concatenate(xs, axis=0)
    return (
        cat(maxima), cat(totals), cat(sums), cat(block_query), cat(block_keys).astype(bf16), product
    )


def local_kernel(groups, frame, x_ref, logit_ref, m_ref, l_ref, a_ref, q_ref, k_ref, map_ref):
    rows = [
        jnp.concatenate([x_ref[s, 0, kind].astype(f32) for s in range(groups)], axis=0)
        for kind in range(4)
    ]
    out = local_head(*rows, logit_ref[0].astype(f32), frame)
    for ref, value in zip((m_ref, l_ref, a_ref, q_ref, k_ref, map_ref), out):
        ref[0] = value


def far_kernel(groups, m_ref, l_ref, a_ref, q_ref, k_ref, v_ref, map_ref, o_ref):
    own = lax.axis_index("ctx")
    scale = q_ref.shape[-1] ** (-0.5)

    def step(i, state):
        top, total, acc, current = state
        at = own - 1 - i
        s = mm_nt(current.astype(bf16), k_ref[at, 0]) * scale
        new = jnp.maximum(top, jnp.max(s, axis=1, keepdims=True))
        factor = jnp.exp(top - new)
        w = jnp.exp(s - new)
        total = total * factor + jnp.sum(w, axis=1, keepdims=True)
        acc = acc * factor + mm(w.astype(bf16), v_ref[at, 0])
        return new, total, acc, wide(current, map_ref[at, 0])

    _, total, acc, _ = lax.fori_loop(0, own, step, (m_ref[0], l_ref[0], a_ref[0], q_ref[0]))
    out = acc / total
    n = out.shape[0] // groups
    for s in range(groups):
        o_ref[s, 0] = out[s * n : (s + 1) * n].astype(bf16)


def shards(queries, key_vectors, values, directions, beta_logit):
    groups = lax.axis_size("head")
    sections = lax.axis_size("ctx")
    local_rows, head_total, width = queries.shape
    heads = head_total // groups
    rows = local_rows * groups
    frame = 2 * SUB

    def outgoing(x):
        return x.reshape(local_rows, groups, heads, width).transpose(1, 2, 0, 3)

    stacked = jnp.stack([outgoing(x) for x in (queries, key_vectors, values, directions)], axis=2)
    arrived = lax.all_to_all(stacked, "head", 0, 0, tiled=True)
    logit = beta_logit.reshape(local_rows, groups, heads).transpose(1, 2, 0)
    logit = lax.all_to_all(logit, "head", 0, 0, tiled=True)
    logit = logit.transpose(1, 0, 2).reshape(heads, 1, rows)
    value_rows = arrived[:, :, 2].transpose(1, 0, 2, 3).reshape(heads, rows, width)
    all_values = lax.all_gather(value_rows, "ctx")

    per_head = lambda *s: pl.BlockSpec((1,) + s, lambda h: (h,) + (0,) * len(s))
    shape = lambda *s: jax.ShapeDtypeStruct((heads,) + s, f32)
    state = pl.pallas_call(
        functools.partial(local_kernel, groups, frame),
        grid=(heads,),
        in_specs=[
            pl.BlockSpec((groups, 1, 4, local_rows, width), lambda h: (0, h, 0, 0, 0)),
            per_head(1, rows),
        ],
        out_specs=[
            per_head(rows, 1), per_head(rows, 1), per_head(rows, width),
            per_head(rows, width), per_head(rows, width), per_head(width, width),
        ],
        out_shape=[
            shape(rows, 1), shape(rows, 1), shape(rows, width), shape(rows, width),
            jax.ShapeDtypeStruct((heads, rows, width), bf16), shape(width, width),
        ],
        name="local_block",
    )(arrived, logit)
    top, total, acc, query, keys, block_map = state
    all_keys = lax.all_gather(keys, "ctx")
    all_maps = lax.all_gather(block_map, "ctx")
    every = lambda *s: pl.BlockSpec((sections, 1) + s, lambda h: (0, h) + (0,) * len(s))
    out = pl.pallas_call(
        functools.partial(far_kernel, groups),
        grid=(heads,),
        in_specs=[
            per_head(rows, 1), per_head(rows, 1), per_head(rows, width), per_head(rows, width),
            every(rows, width), every(rows, width), every(width, width),
        ],
        out_specs=pl.BlockSpec((groups, 1, local_rows, width), lambda h: (0, h, 0, 0)),
        out_shape=jax.ShapeDtypeStruct((groups, heads, local_rows, width), bf16),
        name="far_blocks",
    )(top, total, acc, query, all_keys, all_values, all_maps)
    back = lax.all_to_all(out, "head", 0, 0, tiled=True)
    return back.transpose(2, 0, 1, 3).reshape(local_rows, head_total, width)


def solution(mesh):
    rows = P(("ctx", "head"), None, None)
    in_specs = (rows, rows, rows, rows, P(("ctx", "head"), None))
    return jax.shard_map(shards, mesh=mesh, in_specs=in_specs, out_specs=rows, check_vma=False)
```

time: 649 us -> 340 us (0.52)
  other arithmetic: 256 us -> 1.87 us
  matrix products: 135 us -> 0 us
  waiting for transfers between devices: 102 us -> 207 us
  Pallas kernels: 0 us -> 82.2 us
  starting transfers between devices: 63.8 us -> 8.66 us
  local copies, waits for them, and re-layouts: 56.2 us -> 9.22 us
  loops' own time: 13 us -> 0 us
  between operations: 0.8 us -> 13.2 us
    another operation x2 -> x1, other arithmetic: 237 us -> 1.87 us  [shards(): jnp.stack([outgoing(x) for x in (queries, key_vectors, values, directions...]
    all_gather x0 -> x3, waiting for transfers between devices: none -> 172 us  [the longest x1 65 us: shards(): all_keys = lax.all_gather(keys, 'ctx')]
    dot_general x59 -> x0, matrix products: 131 us -> none  [the longest x10 21.7 us: absorb(): jnp.einsum('ihj,jhe->ihe', weights.astype(jnp.bfloat16), value_entries, p...]
    ppermute x21 -> x0, waiting for transfers between devices: 94.6 us -> none  [from_behind(): return lax.ppermute(value, axis, pairs)]
    pallas_call x0 -> x2, Pallas kernels: none -> 82.2 us  [the longest x1 44.1 us: shards(): pl.pallas_call(functools.partial(far_kernel, groups), grid=(heads,), in_s...]
    ppermute x21 -> x0, starting transfers between devices: 40.3 us -> none  [from_behind(): return lax.ppermute(value, axis, pairs)]
    all_to_all x5 -> x2, waiting for transfers between devices: 6.89 us -> 34.3 us  [the longest x1 34.3 us: shards(): arrived = lax.all_to_all(stacked, 'head', 0, 0, tiled=True)]
    while x64 -> x0, local copies, waits for them, and re-layouts: 25.1 us -> none
  transfers between devices with their start and end apart: 26 -> 5, of which waited for: 24 -> 4; matrix products, arithmetic and copies ran while one was open for 55% -> 2% of each run, Pallas kernels for 0% -> 0%
where the time goes in v1:
time: 340 us; the launch traced here: 334 us
  waiting for transfers between devices  207 us (61%)
  Pallas kernels  82.2 us (24%)
  between operations  13.2 us (4%)
  blocking collectives  11.6 us (3%)
  local copies, waits for them, and re-layouts  9.22 us (3%)
  starting transfers between devices  8.66 us (3%)
    all_gather x1, waiting for transfers between devices, shards(): all_keys = lax.all_gather(keys, 'ctx')  65 us
    all_gather x1, waiting for transfers between devices, shards(): all_values = lax.all_gather(value_rows, 'ctx')  65 us
    pallas_call x1, Pallas kernels, shards(): pl.pallas_call(functools.partial(far_kernel, groups), grid=(heads,), in_s...  44.1 us
    all_gather x1, waiting for transfers between devices, shards(): all_maps = lax.all_gather(block_map, 'ctx')  41.9 us
    pallas_call x1, Pallas kernels, shards(): pl.pallas_call(functools.partial(local_kernel, groups, frame), grid=(head...  38.1 us
    all_to_all x1, waiting for transfers between devices, shards(): arrived = lax.all_to_all(stacked, 'head', 0, 0, tiled=True)  34.3 us
    all_to_all x1, blocking collectives, shards(): back = lax.all_to_all(out, 'head', 0, 0, tiled=True)  11.6 us
  transfers between devices with their start and end apart: 5, of which 4 were waited for; matrix products, arithmetic and copies ran while one was open for 2% of the time, Pallas kernels for 0%

profile of v1, /device:TPU:26, one launch (start us, length us, event | category | flops | bytes accessed | tf_op | source)
XLA Modules:
  0.0 333.6 jit_solution(4377594423151933325)
XLA Ops:
  6.5 0.0 copy-start.1
  6.5 0.0 copy-start.2
  6.5 4.4 %all-to-all-start.1 = ((bf16[4,8,96]{2,1,0:T(8,128)(2,1)}), bf16[4,8,96]{2,1,0:T(8,128)(2,1)S(1)}, u32[]{:S(2)}, u32[]{:S(2)}) async-start(bf16[4,8,96]{2,1,0:T(8,128)(2,1)} %bitcast.43), calls=%async_computation.1 | async-start | bytes 16384 | tf_op jit(solution)/shard_map/all_to_all | solution.py:187
  10.9 1.4 copy.28
  12.4 1.4 copy.29
  13.8 0.0 copy-done.1
  13.8 0.3 copy.30
  14.1 0.0 copy-done.2
  14.1 0.3 copy.31
  14.4 1.9 pad_maximum_fusion
  16.3 0.0 all-to-all-done.1
  16.3 4.2 %all-to-all-start = ((bf16[4,8,4,96,128]{4,3,2,1,0:T(8,128)(2,1)}), bf16[4,8,4,96,128]{4,3,2,1,0:T(8,128)(2,1)S(1)}, u32[]{:S(2)}, u32[]{:S(2)}) async-start(bf16[4,8,4,96,128]{4,3,2,1,0:T(8,128)(2,1)} %pad_maximum_fusion), calls=%async_computation | async-start | bytes 6291456 | tf_op jit(solution)/shard_map/all_to_all | solution.py:185
  20.5 0.0 all-gather.10.cloned.1.call-start
  20.5 0.7 reshape.30.logit_ref
  21.2 34.3 %all-to-all-done.x_ref = bf16[4,8,4,96,128]{4,3,2,1,0:T(8,128)(2,1)S(1)} async-done(((bf16[4,8,4,96,128]{4,3,2,1,0:T(8,128)(2,1)}), bf16[4,8,4,96,128]{4,3,2,1,0:T(8,128)(2,1)S(1)}, u32[]{:S(2)}, u32[]{:S(2)}) %all-to-all-start) | async-done | bytes 3145760 | tf_op jit(solution)/shard_map/all_to_all | solution.py:185
  55.5 0.0 copy-start
  55.5 1.7 copy-done
  57.2 38.1 %local_block.1 = (f32[8,384,1]{2,1,0:T(8,128)}, f32[8,384,1]{2,1,0:T(8,128)}, f32[8,384,128]{2,1,0:T(8,128)}, f32[8,384,128]{2,1,0:T(8,128)}, bf16[8,384,128]{2,1,0:T(8,128)(2,1)}, /*index=5*/f32[8,128,128]{2,1,0:T(8,128)}) custom-call(bf16[4,8,4,96,128]{4,3,2,1,0:T(8,128)(2,1)} %copy-done, bf16[8,1,384]{2,1,0:T(2,128)(2,1)} %reshape.30.logit_ref), custom_call_target="tpu_custom_call" | custom-call | tf_op jit(solution)/shard_map/local_block/pallas_call | solution.py:194
  95.3 0.0 all-gather.10.cloned.1.call-update
  95.3 0.0 all-gather.6.cloned.1.call-start
  95.3 1.2 slice_bitcast_fusion
  96.6 1.0 copy.34
  97.5 0.0 all-gather.6.cloned.1.call-update
  97.6 0.0 all-gather.8.cloned.1.call-start
  97.6 0.7 all-gather.8.cloned.1.call-update
  98.3 41.9 %all-gather.10.cloned.1.call-done = f32[64,128,128]{2,1,0:T(8,128)} async-done(((f32[8,128,128]{2,1,0:T(8,128)}), f32[64,128,128]{2,1,0:T(8,128)}) %all-gather.10.cloned.1.call-update) | async-done | bytes 4194320 | tf_op jit(solution)/shard_map/all_gather | solution.py:213
  140.2 65.0 %all-gather.6.cloned.1.call-done.v_ref = bf16[8,8,384,128]{3,2,1,0:T(8,128)(2,1)} async-done(((bf16[1,8,384,128]{3,2,1,0:T(8,128)(2,1)}), bf16[8,8,384,128]{3,2,1,0:T(8,128)(2,1)}) %all-gather.6.cloned.1.call-update) | async-done | bytes 6291472 | tf_op jit(solution)/shard_map/all_gather | solution.py:190
  205.1 65.0 %all-gather.8.cloned.1.call-done = bf16[64,384,128]{2,1,0:T(8,128)(2,1)} async-done(((bf16[8,384,128]{2,1,0:T(8,128)(2,1)}), bf16[64,384,128]{2,1,0:T(8,128)(2,1)}) %all-gather.8.cloned.1.call-update) | async-done | bytes 6291472 | tf_op jit(solution)/shard_map/all_gather | solution.py:212
  270.2 44.1 %far_blocks.1 = bf16[4,8,96,128]{3,2,1,0:T(8,128)(2,1)} custom-call(f32[8,384,1]{2,1,0:T(8,128)} %get-tuple-element.11.m_ref, f32[8,384,1]{2,1,0:T(8,128)} %get-tuple-element.12.l_ref, f32[8,384,128]{2,1,0:T(8,128)} %get-tuple-element.13.a_ref, f32[8,384,128]{2,1,0:T(8,128)} %get-tuple-element.14.q_ref, bf16[8,8,384,128]{3,2,1,0:T(8,128)(2,1)} %bitcast.34, ...), custom_call_target="tpu_custom_call" | custom-call | tf_op jit(solution)/shard_map/far_blocks/pallas_call | solution.py:215
  314.2 11.6 %all_to_all.15 = bf16[4,8,96,128]{3,2,1,0:T(8,128)(2,1)S(1)} all-to-all(bf16[4,8,96,128]{3,2,1,0:T(8,128)(2,1)} %far_blocks.1), channel_id=1, replica_groups=mesh['ctx'=8,'head'=4] {'head'}, dimensions={0} | all-to-all | bytes 1572864 | tf_op jit(solution)/shard_map/all_to_all | solution.py:226
  325.9 1.2 copy.35
  (1 shorter events, 0.0 us)
Async XLA Ops:
  6.5 7.3 %copy-start.1 = (bf16[96,32,128]{2,1,0:T(8,128)(2,1)S(1)}, bf16[96,32,128]{2,1,0:T(8,128)(2,1)}, u32[]{:S(2)}) copy-start(bf16[96,32,128]{2,1,0:T(8,128)(2,1)} %param.7) | copy-start | bytes 2359300
  6.5 7.6 %copy-start.2 = (bf16[96,32,128]{2,1,0:T(8,128)(2,1)S(1)}, bf16[96,32,128]{2,1,0:T(8,128)(2,1)}, u32[]{:S(2)}) copy-start(bf16[96,32,128]{2,1,0:T(8,128)(2,1)} %param.8) | copy-start | bytes 2359300
  6.5 9.8 %all-to-all-start.1 = ((bf16[4,8,96]{2,1,0:T(8,128)(2,1)}), bf16[4,8,96]{2,1,0:T(8,128)(2,1)S(1)}, u32[]{:S(2)}, u32[]{:S(2)}) async-start(bf16[4,8,96]{2,1,0:T(8,128)(2,1)} %bitcast.43), calls=%async_computation.1 | async-start | bytes 16384 | tf_op jit(solution)/shard_map/all_to_all | solution.py:187
  16.3 39.2 %all-to-all-start = ((bf16[4,8,4,96,128]{4,3,2,1,0:T(8,128)(2,1)}), bf16[4,8,4,96,128]{4,3,2,1,0:T(8,128)(2,1)S(1)}, u32[]{:S(2)}, u32[]{:S(2)}) async-start(bf16[4,8,4,96,128]{4,3,2,1,0:T(8,128)(2,1)} %pad_maximum_fusion), calls=%async_computation | async-start | bytes 6291456 | tf_op jit(solution)/shard_map/all_to_all | solution.py:185
  20.5 119.6 %all-gather.10.cloned.1.call-start = ((), (), s32[]{:S(2)}) async-start(), calls=%async_computation.5 | async-start | bytes 4718592 | tf_op jit(solution)/shard_map/all_gather | solution.py:213
  55.5 1.7 copy-start
  95.3 109.8 %all-gather.6.cloned.1.call-start = ((), (), s32[]{:S(2)}) async-start(), calls=%async_computation.3 | async-start | bytes 7077888 | tf_op jit(solution)/shard_map/all_gather | solution.py:190
  97.6 172.6 %all-gather.8.cloned.1.call-start = ((), (), s32[]{:S(2)}) async-start(), calls=%async_computation.4 | async-start | bytes 7077888 | tf_op jit(solution)/shard_map/all_gather | solution.py:212
Sparse Core Ops, SparseCore 0:
  95.4 44.7 all-gather.9
  141.8 63.2 all-gather.5
  206.8 63.3 all-gather.7

commit v2 on v1

--- a/solution.py
+++ b/solution.py
@@ -134,49 +134,275 @@
         block_keys.append(moved)
     cat = lambda xs: jnp.concatenate(xs, axis=0)
     return (
-        cat(maxima), cat(totals), cat(sums), cat(block_query), cat(block_keys).astype(bf16), product
+        cat(maxima), cat(totals), cat(sums), cat(block_query), cat(block_keys), product
     )
 
 
-def local_kernel(groups, frame, x_ref, logit_ref, m_ref, l_ref, a_ref, q_ref, k_ref, map_ref):
-    rows = [
-        jnp.concatenate([x_ref[s, 0, kind].astype(f32) for s in range(groups)], axis=0)
-        for kind in range(4)
-    ]
-    out = local_head(*rows, logit_ref[0].astype(f32), frame)
-    for ref, value in zip((m_ref, l_ref, a_ref, q_ref, k_ref, map_ref), out):
-        ref[0] = value
-
-
-def far_kernel(groups, m_ref, l_ref, a_ref, q_ref, k_ref, v_ref, map_ref, o_ref):
+KEYS, VALUES, MAPS = 0, 1, 2
+MESH = pl.DeviceIdType.MESH
+
+
+def block_kernel(
+    groups, levels, frame, x_ref, v_ref, logit_ref, o_ref,
+    kv_buf, map_buf, key_self, key_wide, query, acc, top, total, own_map, side_map,
+    send_on, send_side, arrive, pair_send, pair_arrive,
+):
+    heads, rows, width = v_ref.shape
+    part = map_buf.shape[2]
+    scale = width ** (-0.5)
     own = lax.axis_index("ctx")
-    scale = q_ref.shape[-1] ** (-0.5)
-
-    def step(i, state):
-        top, total, acc, current = state
-        at = own - 1 - i
-        s = mm_nt(current.astype(bf16), k_ref[at, 0]) * scale
-        new = jnp.maximum(top, jnp.max(s, axis=1, keepdims=True))
-        factor = jnp.exp(top - new)
-        w = jnp.exp(s - new)
-        total = total * factor + jnp.sum(w, axis=1, keepdims=True)
-        acc = acc * factor + mm(w.astype(bf16), v_ref[at, 0])
-        return new, total, acc, wide(current, map_ref[at, 0])
-
-    _, total, acc, _ = lax.fori_loop(0, own, step, (m_ref[0], l_ref[0], a_ref[0], q_ref[0]))
-    out = acc / total
-    n = out.shape[0] // groups
-    for s in range(groups):
-        o_ref[s, 0] = out[s * n : (s + 1) * n].astype(bf16)
+    level = own // 2
+    core = own % 2
+    onward, back, side = own + 2, own - 2, own + 1 - 2 * core
+    has_next = level < levels - 1
+    has_map = has_next & (level >= 1)
+    barrier = pltpu.get_barrier_semaphore()
+
+    def greet(at):
+        pl.semaphore_signal(barrier, inc=1, device_id={"ctx": at}, device_id_type=MESH)
+
+    greet(side)
+
+    @pl.when(has_next)
+    def _():
+        greet(onward)
+
+    @pl.when(level >= 1)
+    def _():
+        greet(back)
+
+    pl.semaphore_wait(barrier, 1 + has_next.astype(jnp.int32) + (level >= 1).astype(jnp.int32))
+
+    def slot(at, column, kind):
+        return map_buf.at[at, column] if kind == MAPS else kv_buf.at[at, column, kind]
+
+    def copy(source, at, kind, target, send):
+        return pltpu.make_async_remote_copy(
+            src_ref=source,
+            dst_ref=slot(at, core, kind),
+            send_sem=send.at[at, kind],
+            recv_sem=arrive.at[at, core, kind],
+            device_id={"ctx": target},
+            device_id_type=MESH,
+        )
+
+    def send_next(source, at, kind):
+        copy(source, at, kind, onward, send_on).start()
+
+    def await_slot(at, column, kind):
+        pltpu.make_async_remote_copy(
+            src_ref=slot(at, column, kind),
+            dst_ref=slot(at, column, kind),
+            send_sem=send_side.at[at, kind],
+            recv_sem=arrive.at[at, column, kind],
+            device_id={"ctx": side},
+            device_id_type=MESH,
+        ).wait_recv()
+
+    def relay(at, kind):
+        await_slot(at, core, kind)
+
+        @pl.when(has_next)
+        def _():
+            send_next(slot(at, core, kind), at, kind)
+
+        copy(slot(at, core, kind), at, kind, side, send_side).start()
+
+    @pl.when(has_next)
+    def _():
+        send_next(v_ref, level, VALUES)
+
+    @pl.when(core == 0)
+    def _():
+        copy(v_ref, level, VALUES, side, send_side).start()
+
+    def local(h, carry):
+        pieces = [
+            jnp.concatenate([x_ref[s, h, kind].astype(f32) for s in range(groups)], axis=0)
+            for kind in range(4)
+        ]
+        m, l, a, q, k, moved = local_head(*pieces, logit_ref[h].astype(f32), frame)
+        top[h] = m
+        total[h] = l
+        acc[h] = a
+        query[h] = q
+        key_wide[h] = k
+        key_self[h] = k.astype(bf16)
+        own_map[h] = moved
+        return carry
+
+    lax.fori_loop(0, heads // 2, local, 0)
+
+    @pl.when(level >= 1)
+    def _():
+        relay(level - 1, VALUES)
+
+    lax.fori_loop(heads // 2, heads, local, 0)
+
+    swap = pltpu.make_async_remote_copy(
+        src_ref=own_map,
+        dst_ref=side_map,
+        send_sem=pair_send,
+        recv_sem=pair_arrive,
+        device_id={"ctx": side},
+        device_id_type=MESH,
+    )
+    swap.start()
+
+    @pl.when((core == 1) & has_next)
+    def _():
+        send_next(key_self, level, KEYS)
+
+    @pl.when(core == 0)
+    def _():
+        copy(key_self, level, KEYS, side, send_side).start()
+
+    @pl.when(level >= 2)
+    def _():
+        relay(level - 2, VALUES)
+
+    swap.wait_recv()
+
+    @pl.when((core == 0) & has_next)
+    def _():
+        def rebase(h, carry):
+            kv_buf[level, 0, KEYS, h] = wide_nt(key_wide[h], side_map[h]).astype(bf16)
+            return carry
+
+        lax.fori_loop(0, heads, rebase, 0)
+        send_next(slot(level, 0, KEYS), level, KEYS)
+
+    @pl.when(has_map & (core == 0))
+    def _():
+        for i in range(part):
+            map_buf[level, 0, i] = wide(side_map[i], own_map[i])
+
+    @pl.when(has_map & (core == 1))
+    def _():
+        for i in range(part):
+            map_buf[level, 1, i] = wide(own_map[part + i], side_map[part + i])
+
+    @pl.when(has_map)
+    def _():
+        send_next(slot(level, core, MAPS), level, MAPS)
+
+    def absorb(h, pieces):
+        current = query[h].astype(bf16)
+        scores = [mm_nt(current, kv_buf[at, c, KEYS, h]) * scale for at, c in pieces]
+        new = top[h]
+        for s in scores:
+            new = jnp.maximum(new, jnp.max(s, axis=1, keepdims=True))
+        factor = jnp.exp(top[h] - new)
+        amount = total[h] * factor
+        weighted = acc[h] * factor
+        for s, (at, c) in zip(scores, pieces):
+            w = jnp.exp(s - new)
+            amount = amount + jnp.sum(w, axis=1, keepdims=True)
+            weighted = weighted + mm(w.astype(bf16), kv_buf[at, c, VALUES, h])
+        top[h] = new
+        total[h] = amount
+        acc[h] = weighted
+
+    @pl.when(core == 1)
+    def _():
+        await_slot(level, 0, VALUES)
+        await_slot(level, 0, KEYS)
+
+        def near(h, carry):
+            absorb(h, [(level, 0)])
+            query[h] = wide(query[h], side_map[h])
+            return carry
+
+        lax.fori_loop(0, heads, near, 0)
+
+    def far(i, carry):
+        at = level - 1 - i
+
+        @pl.when(i >= 2)
+        def _():
+            relay(at, VALUES)
+
+        relay(at, KEYS)
+
+        @pl.when(at >= 1)
+        def _():
+            relay(at, MAPS)
+
+        await_slot(at, 1 - core, VALUES)
+        await_slot(at, 1 - core, KEYS)
+
+        def one(h, inner):
+            absorb(h, [(at, 1), (at, 0)])
+            return inner
+
+        lax.fori_loop(0, heads, one, 0)
+
+        @pl.when(at >= 1)
+        def _():
+            await_slot(at, 1 - core, MAPS)
+
+            def move(h, inner):
+                query[h] = wide(query[h], map_buf[at, h // part, h % part])
+                return inner
+
+            lax.fori_loop(0, heads, move, 0)
+
+        return carry
+
+    lax.fori_loop(0, level, far, 0)
+
+    def finish(h, carry):
+        out = acc[h] / total[h]
+        n = rows // groups
+        for s in range(groups):
+            o_ref[s, h] = out[s * n : (s + 1) * n].astype(bf16)
+        return carry
+
+    lax.fori_loop(0, heads, finish, 0)
+
+    def settle(at, kind, target, send):
+        copy(slot(at, core, kind), at, kind, target, send).wait_send()
+
+    def settle_side(at, carry):
+        settle(at, KEYS, side, send_side)
+        settle(at, VALUES, side, send_side)
+
+        @pl.when(at >= 1)
+        def _():
+            settle(at, MAPS, side, send_side)
+
+        return carry
+
+    def settle_next(at, carry):
+        settle(at, KEYS, onward, send_on)
+        settle(at, VALUES, onward, send_on)
+
+        @pl.when(at >= 1)
+        def _():
+            settle(at, MAPS, onward, send_on)
+
+        return carry
+
+    lax.fori_loop(0, level, settle_side, 0)
+
+    @pl.when(core == 0)
+    def _():
+        settle(level, KEYS, side, send_side)
+        settle(level, VALUES, side, send_side)
+
+    @pl.when(has_next)
+    def _():
+        lax.fori_loop(0, level + 1, settle_next, 0)
+
+    swap.wait_send()
 
 
 def shards(queries, key_vectors, values, directions, beta_logit):
     groups = lax.axis_size("head")
-    sections = lax.axis_size("ctx")
+    levels = lax.axis_size("ctx") // 2
     local_rows, head_total, width = queries.shape
     heads = head_total // groups
     rows = local_rows * groups
-    frame = 2 * SUB
 
     def outgoing(x):
         return x.reshape(local_rows, groups, heads, width).transpose(1, 2, 0, 3)
@@ -187,42 +413,33 @@
     logit = lax.all_to_all(logit, "head", 0, 0, tiled=True)
     logit = logit.transpose(1, 0, 2).reshape(heads, 1, rows)
     value_rows = arrived[:, :, 2].transpose(1, 0, 2, 3).reshape(heads, rows, width)
-    all_values = lax.all_gather(value_rows, "ctx")
-
-    per_head = lambda *s: pl.BlockSpec((1,) + s, lambda h: (h,) + (0,) * len(s))
-    shape = lambda *s: jax.ShapeDtypeStruct((heads,) + s, f32)
-    state = pl.pallas_call(
-        functools.partial(local_kernel, groups, frame),
-        grid=(heads,),
-        in_specs=[
-            pl.BlockSpec((groups, 1, 4, local_rows, width), lambda h: (0, h, 0, 0, 0)),
-            per_head(1, rows),
+    part = heads // 2
+    vmem = pl.BlockSpec(memory_space=pltpu.VMEM)
+    out = pl.pallas_call(
+        functools.partial(block_kernel, groups, levels, 2 * SUB),
+        in_specs=[vmem] * 3,
+        out_specs=vmem,
+        out_shape=jax.ShapeDtypeStruct((groups, heads, local_rows, width), bf16),
+        scratch_shapes=[
+            pltpu.VMEM((levels, 2, 2, heads, rows, width), bf16),
+            pltpu.VMEM((levels, 2, part, width, width), f32),
+            pltpu.VMEM((heads, rows, width), bf16),
+            pltpu.VMEM((heads, rows, width), f32),
+            pltpu.VMEM((heads, rows, width), f32),
+            pltpu.VMEM((heads, rows, width), f32),
+            pltpu.VMEM((heads, rows, 1), f32),
+            pltpu.VMEM((heads, rows, 1), f32),
+            pltpu.VMEM((heads, width, width), f32),
+            pltpu.VMEM((heads, width, width), f32),
+            pltpu.SemaphoreType.DMA((levels, 3)),
+            pltpu.SemaphoreType.DMA((levels, 3)),
+            pltpu.SemaphoreType.DMA((levels, 2, 3)),
+            pltpu.SemaphoreType.DMA,
+            pltpu.SemaphoreType.DMA,
         ],
-        out_specs=[
-            per_head(rows, 1), per_head(rows, 1), per_head(rows, width),
-            per_head(rows, width), per_head(rows, width), per_head(width, width),
-        ],
-        out_shape=[
-            shape(rows, 1), shape(rows, 1), shape(rows, width), shape(rows, width),
-            jax.ShapeDtypeStruct((heads, rows, width), bf16), shape(width, width),
-        ],
-        name="local_block",
-    )(arrived, logit)
-    top, total, acc, query, keys, block_map = state
-    all_keys = lax.all_gather(keys, "ctx")
-    all_maps = lax.all_gather(block_map, "ctx")
-    every = lambda *s: pl.BlockSpec((sections, 1) + s, lambda h: (0, h) + (0,) * len(s))
-    out = pl.pallas_call(
-        functools.partial(far_kernel, groups),
-        grid=(heads,),
-        in_specs=[
-            per_head(rows, 1), per_head(rows, 1), per_head(rows, width), per_head(rows, width),
-            every(rows, width), every(rows, width), every(width, width),
-        ],
-        out_specs=pl.BlockSpec((groups, 1, local_rows, width), lambda h: (0, h, 0, 0)),
-        out_shape=jax.ShapeDtypeStruct((groups, heads, local_rows, width), bf16),
-        name="far_blocks",
-    )(top, total, acc, query, all_keys, all_values, all_maps)
+        compiler_params=pltpu.CompilerParams(collective_id=0, has_side_effects=True),
+        name="block_chain",
+    )(arrived, value_rows, logit)
     back = lax.all_to_all(out, "head", 0, 0, tiled=True)
     return back.transpose(2, 0, 1, 3).reshape(local_rows, head_total, width)
 

time: 340 us -> 196 us (0.58); the launches traced: 334 us -> 194 us
  waiting for transfers between devices: 207 us -> 34.3 us
  Pallas kernels: 82.2 us -> 128 us
  between operations: 13.2 us -> 0.05 us
    all_gather x3 -> x0, waiting for transfers between devices: 172 us -> none  [the longest x1 65 us: shards(): all_keys = lax.all_gather(keys, 'ctx')]
    pallas_call x2 -> x1, Pallas kernels: 82.2 us -> 128 us  [shards(): pl.pallas_call(functools.partial(block_kernel, groups, levels, 2 * SUB),...]
  transfers between devices with their start and end apart: 5 -> 2, of which waited for: 4 -> 1; matrix products, arithmetic and copies ran while one was open for 2% -> 3% of each run, Pallas kernels for 0% -> 0%
where the time goes in v2:
time: 196 us; the launch traced here: 194 us
  Pallas kernels  128 us (65%)
  waiting for transfers between devices  34.3 us (17%)
  blocking collectives  14.5 us (7%)
  starting transfers between devices  8.57 us (4%)
  local copies, waits for them, and re-layouts  7.26 us (4%)
    pallas_call x1, Pallas kernels, shards(): pl.pallas_call(functools.partial(block_kernel, groups, levels, 2 * SUB),...  128 us
    all_to_all x1, waiting for transfers between devices, shards(): arrived = lax.all_to_all(stacked, 'head', 0, 0, tiled=True)  34.3 us
    all_to_all x1, blocking collectives, shards(): back = lax.all_to_all(out, 'head', 0, 0, tiled=True)  14.5 us
    all_to_all x1, starting transfers between devices, shards(): logit = lax.all_to_all(logit, 'head', 0, 0, tiled=True)  4.38 us
    unnamed x10, local copies, waits for them, and re-layouts  4.28 us
    all_to_all x1, starting transfers between devices, shards(): arrived = lax.all_to_all(stacked, 'head', 0, 0, tiled=True)  4.19 us
  transfers between devices with their start and end apart: 2, of which 1 were waited for; matrix products, arithmetic and copies ran while one was open for 3% of the time, Pallas kernels for 0%

profile of v2, /device:TPU:26, one launch (start us, length us, event | category | flops | bytes accessed | tf_op | source)
XLA Modules:
  0.0 194.2 jit_solution(18005988561337236690)
XLA Ops:
  0.0 0.0 copy-start.1
  0.0 0.0 copy-start.2
  0.0 4.4 %all-to-all-start.1 = ((bf16[4,8,96]{2,1,0:T(8,128)(2,1)}), bf16[4,8,96]{2,1,0:T(8,128)(2,1)S(1)}, u32[]{:S(2)}, u32[]{:S(2)}) async-start(bf16[4,8,96]{2,1,0:T(8,128)(2,1)} %bitcast.39), calls=%async_computation.1 | async-start | bytes 16384 | tf_op jit(solution)/shard_map/all_to_all | solution.py:413
  4.4 1.4 copy.24
  5.8 1.4 copy.21
  7.3 0.0 copy-done.1
  7.3 0.3 copy.22
  7.6 0.0 copy-done.2
  7.6 0.3 copy.23
  7.9 1.9 pad_maximum_fusion
  9.8 0.0 all-to-all-done.1
  9.8 4.2 %all-to-all-start = ((bf16[4,8,4,96,128]{4,3,2,1,0:T(8,128)(2,1)}), bf16[4,8,4,96,128]{4,3,2,1,0:T(8,128)(2,1)S(1)}, u32[]{:S(2)}, u32[]{:S(2)}) async-start(bf16[4,8,4,96,128]{4,3,2,1,0:T(8,128)(2,1)} %pad_maximum_fusion), calls=%async_computation | async-start | bytes 6291456 | tf_op jit(solution)/shard_map/all_to_all | solution.py:411
  14.0 0.7 reshape.32.logit_ref
  14.7 34.3 %all-to-all-done.x_ref = bf16[4,8,4,96,128]{4,3,2,1,0:T(8,128)(2,1)S(1)} async-done(((bf16[4,8,4,96,128]{4,3,2,1,0:T(8,128)(2,1)}), bf16[4,8,4,96,128]{4,3,2,1,0:T(8,128)(2,1)S(1)}, u32[]{:S(2)}, u32[]{:S(2)}) %all-to-all-start) | async-done | bytes 3145760 | tf_op jit(solution)/shard_map/all_to_all | solution.py:411
  49.0 0.0 copy-start
  49.0 0.1 slice_bitcast_fusion
  49.0 1.0 copy.25
  50.1 0.8 copy-done
  50.9 127.7 %block_chain.1 = bf16[4,8,96,128]{3,2,1,0:T(8,128)(2,1)} custom-call(bf16[4,8,4,96,128]{4,3,2,1,0:T(8,128)(2,1)} %copy-done, bf16[8,384,128]{2,1,0:T(8,128)(2,1)} %bitcast.37, bf16[8,1,384]{2,1,0:T(2,128)(2,1)} %reshape.32.logit_ref), custom_call_target="tpu_custom_call" | custom-call | tf_op jit(solution)/shard_map/block_chain/pallas_call | solution.py:418
  178.5 14.5 %all_to_all.15 = bf16[4,8,96,128]{3,2,1,0:T(8,128)(2,1)S(1)} all-to-all(bf16[4,8,96,128]{3,2,1,0:T(8,128)(2,1)} %block_chain.1), channel_id=1, replica_groups=mesh['ctx'=8,'head'=4] {'head'}, dimensions={0} | all-to-all | bytes 1572864 | tf_op jit(solution)/shard_map/all_to_all | solution.py:443
  193.0 1.2 copy.28
  (1 shorter events, 0.0 us)
Async XLA Ops:
  0.0 7.3 %copy-start.1 = (bf16[96,32,128]{2,1,0:T(8,128)(2,1)S(1)}, bf16[96,32,128]{2,1,0:T(8,128)(2,1)}, u32[]{:S(2)}) copy-start(bf16[96,32,128]{2,1,0:T(8,128)(2,1)} %param.6) | copy-start | bytes 2359300
  0.0 7.6 %copy-start.2 = (bf16[96,32,128]{2,1,0:T(8,128)(2,1)S(1)}, bf16[96,32,128]{2,1,0:T(8,128)(2,1)}, u32[]{:S(2)}) copy-start(bf16[96,32,128]{2,1,0:T(8,128)(2,1)} %param.7) | copy-start | bytes 2359300
  0.0 9.8 %all-to-all-start.1 = ((bf16[4,8,96]{2,1,0:T(8,128)(2,1)}), bf16[4,8,96]{2,1,0:T(8,128)(2,1)S(1)}, u32[]{:S(2)}, u32[]{:S(2)}) async-start(bf16[4,8,96]{2,1,0:T(8,128)(2,1)} %bitcast.39), calls=%async_computation.1 | async-start | bytes 16384 | tf_op jit(solution)/shard_map/all_to_all | solution.py:413
  9.8 39.2 %all-to-all-start = ((bf16[4,8,4,96,128]{4,3,2,1,0:T(8,128)(2,1)}), bf16[4,8,4,96,128]{4,3,2,1,0:T(8,128)(2,1)S(1)}, u32[]{:S(2)}, u32[]{:S(2)}) async-start(bf16[4,8,4,96,128]{4,3,2,1,0:T(8,128)(2,1)} %pad_maximum_fusion), calls=%async_computation | async-start | bytes 6291456 | tf_op jit(solution)/shard_map/all_to_all | solution.py:411
  49.0 1.9 copy-start

commit v3 on v2

--- a/solution.py
+++ b/solution.py
@@ -49,7 +49,7 @@
     return mm(jnp.concatenate([ah, al], axis=1), jnp.concatenate([b_half, b_half], axis=0))
 
 
-def local_head(q_all, k_all, v_all, d_all, logit_row, frame):
+def local_head(q_all, k_all, v_all, d_all, logit_col, frame):
     rows, width = q_all.shape
     count = rows // frame
     scale = width ** (-0.5)
@@ -62,10 +62,7 @@
     def to_row(col):
         return jnp.sum(jnp.where(diagonal, col, 0.0), axis=0, keepdims=True)
 
-    def to_col(row):
-        return jnp.sum(jnp.where(diagonal, row, 0.0), axis=1, keepdims=True)
-
-    rate_row = 2.0 / (1.0 + jnp.exp(-logit_row))
+    rate_col = 2.0 / (1.0 + jnp.exp(-logit_col))
     q, k, v, d, strict, inverse, left, right = [], [], [], [], [], [], [], []
     for f in range(count):
         at = slice(f * frame, (f + 1) * frame)
@@ -73,11 +70,11 @@
         d32 = d_all[at]
         s = lax.rsqrt(jnp.sum(d32 * d32, axis=1, keepdims=True) + 1e-06)
         s_row = to_row(s)
-        rate = rate_row[:, at]
+        rate = rate_col[at]
         gram = mm_nt(df, df)
-        near = jnp.where(below, gram * (to_col(rate) * s) * s_row, 0.0)
+        near = jnp.where(below, gram * (rate * s) * s_row, 0.0)
         q.append(qf), k.append(kf), v.append(vf), d.append(df)
-        strict.append(near), left.append(s), right.append(rate * s_row)
+        strict.append(near), left.append(s), right.append(to_row(rate * s))
         inverse.append(eye - jnp.where((row_at // 2) == (col_at // 2), near, 0.0))
     size = 2
     while size < frame:
@@ -143,14 +140,19 @@
 
 
 def block_kernel(
-    groups, levels, frame, x_ref, v_ref, logit_ref, o_ref,
-    kv_buf, map_buf, key_self, key_wide, query, acc, top, total, own_map, side_map,
+    groups, levels, frame, chunks, x_ref, v_ref, logit_ref, o_ref,
+    x_in, logit_in, out_buf,
+    key_buf, value_buf, map_buf, key_self, key_wide, query, acc, top, total, own_map, side_map,
     send_on, send_side, arrive, pair_send, pair_arrive,
+    x_send, x_arrive, v_send, v_arrive, b_send, b_arrive, o_send, o_arrive, keep,
 ):
-    heads, rows, width = v_ref.shape
+    _, heads, local_rows, width = v_ref.shape
+    rows = groups * local_rows
+    chunk = heads // chunks
     part = map_buf.shape[2]
     scale = width ** (-0.5)
     own = lax.axis_index("ctx")
+    me = lax.axis_index("head")
     level = own // 2
     core = own % 2
     onward, back, side = own + 2, own - 2, own + 1 - 2 * core
@@ -171,10 +173,68 @@
     def _():
         greet(back)
 
-    pl.semaphore_wait(barrier, 1 + has_next.astype(jnp.int32) + (level >= 1).astype(jnp.int32))
+    for p in range(1, groups):
+        peer = (me + p) % groups
+        pl.semaphore_signal(barrier, inc=1, device_id={"head": peer}, device_id_type=MESH)
+    pl.semaphore_wait(
+        barrier, groups + has_next.astype(jnp.int32) + (level >= 1).astype(jnp.int32)
+    )
+
+    def across(source, target, p, send, recv):
+        return pltpu.make_async_remote_copy(
+            src_ref=source,
+            dst_ref=target,
+            send_sem=send,
+            recv_sem=recv,
+            device_id={"head": (me + p) % groups},
+            device_id_type=MESH,
+        )
+
+    def v_copy(p):
+        to = value_buf.at[level, core, :, me]
+        return across(v_ref.at[(me + p) % groups], to, p, v_send.at[p], v_arrive.at[p])
+
+    def b_copy(p):
+        to = logit_in.at[me]
+        return across(logit_ref.at[(me + p) % groups], to, p, b_send.at[p], b_arrive.at[p])
+
+    def x_copy(p, c):
+        at = pl.ds(c * chunk, chunk)
+        source = x_ref.at[(me + p) % groups, at]
+        return across(source, x_in.at[me, at], p, x_send.at[p, c], x_arrive.at[p, c])
+
+    def o_copy(p, h):
+        source = out_buf.at[(me + p) % groups, h]
+        return across(source, o_ref.at[me, h], p, o_send.at[p, h], o_arrive.at[p, h])
+
+    kept = [
+        pltpu.make_async_copy(v_ref.at[me], value_buf.at[level, core, :, me], keep.at[0]),
+        pltpu.make_async_copy(logit_ref.at[me], logit_in.at[me], keep.at[1]),
+        pltpu.make_async_copy(x_ref.at[me], x_in.at[me], keep.at[2]),
+    ]
+    for p in range(1, groups):
+        b_copy(p).start()
+        v_copy(p).start()
+    for c in range(chunks):
+        for p in range(1, groups):
+            x_copy(p, c).start()
+    for one_copy in kept:
+        one_copy.start()
+    for p in range(1, groups):
+        b_copy(p).wait_recv()
+        v_copy(p).wait_recv()
+    for one_copy in kept:
+        one_copy.wait()
+    v_own = value_buf.at[level, core]
+
+    def value_rows(at, c, h):
+        if local_rows % 16 == 0:
+            return value_buf[at, c, h].reshape(rows, width)
+        pieces = [value_buf[at, c, h, s].astype(f32) for s in range(groups)]
+        return jnp.concatenate(pieces, axis=0).astype(bf16)
 
     def slot(at, column, kind):
-        return map_buf.at[at, column] if kind == MAPS else kv_buf.at[at, column, kind]
+        return (key_buf, value_buf, map_buf)[kind].at[at, column]
 
     def copy(source, at, kind, target, send):
         return pltpu.make_async_remote_copy(
@@ -210,18 +270,26 @@
 
     @pl.when(has_next)
     def _():
-        send_next(v_ref, level, VALUES)
+        send_next(v_own, level, VALUES)
 
     @pl.when(core == 0)
     def _():
-        copy(v_ref, level, VALUES, side, send_side).start()
+        copy(v_own, level, VALUES, side, send_side).start()
+
+    at_row = lax.broadcasted_iota(jnp.int32, (local_rows, local_rows), 0)
+    at_col = lax.broadcasted_iota(jnp.int32, (local_rows, local_rows), 1)
+
+    def upright(row):
+        return jnp.sum(jnp.where(at_row == at_col, row, 0.0), axis=1, keepdims=True)
 
     def local(h, carry):
-        pieces = [
-            jnp.concatenate([x_ref[s, h, kind].astype(f32) for s in range(groups)], axis=0)
-            for kind in range(4)
+        joined = lambda xs: jnp.concatenate(xs, axis=0)
+        q0, k0, d0 = [
+            joined([x_in[s, h, kind].astype(f32) for s in range(groups)]) for kind in range(3)
         ]
-        m, l, a, q, k, moved = local_head(*pieces, logit_ref[h].astype(f32), frame)
+        v0 = value_rows(level, core, h)
+        logit = joined([upright(logit_in[s, pl.ds(h, 1), :]) for s in range(groups)])
+        m, l, a, q, k, moved = local_head(q0, k0, v0, d0, logit, frame)
         top[h] = m
         total[h] = l
         acc[h] = a
@@ -231,13 +299,15 @@
         own_map[h] = moved
         return carry
 
-    lax.fori_loop(0, heads // 2, local, 0)
-
-    @pl.when(level >= 1)
-    def _():
-        relay(level - 1, VALUES)
-
-    lax.fori_loop(heads // 2, heads, local, 0)
+    for c in range(chunks):
+        for p in range(1, groups):
+            x_copy(p, c).wait_recv()
+        lax.fori_loop(c * chunk, (c + 1) * chunk, local, 0)
+        if c == (chunks - 1) // 2:
+
+            @pl.when(level >= 1)
+            def _():
+                relay(level - 1, VALUES)
 
     swap = pltpu.make_async_remote_copy(
         src_ref=own_map,
@@ -266,7 +336,7 @@
     @pl.when((core == 0) & has_next)
     def _():
         def rebase(h, carry):
-            kv_buf[level, 0, KEYS, h] = wide_nt(key_wide[h], side_map[h]).astype(bf16)
+            key_buf[level, 0, h] = wide_nt(key_wide[h], side_map[h]).astype(bf16)
             return carry
 
         lax.fori_loop(0, heads, rebase, 0)
@@ -288,7 +358,7 @@
 
     def absorb(h, pieces):
         current = query[h].astype(bf16)
-        scores = [mm_nt(current, kv_buf[at, c, KEYS, h]) * scale for at, c in pieces]
+        scores = [mm_nt(current, key_buf[at, c, h]) * scale for at, c in pieces]
         new = top[h]
         for s in scores:
             new = jnp.maximum(new, jnp.max(s, axis=1, keepdims=True))
@@ -298,10 +368,27 @@
         for s, (at, c) in zip(scores, pieces):
             w = jnp.exp(s - new)
             amount = amount + jnp.sum(w, axis=1, keepdims=True)
-            weighted = weighted + mm(w.astype(bf16), kv_buf[at, c, VALUES, h])
+            weighted = weighted + mm(w.astype(bf16), value_rows(at, c, h))
         top[h] = new
         total[h] = amount
         acc[h] = weighted
+
+    def finish(h):
+        out = acc[h] / total[h]
+        for s in range(groups):
+            piece = out[s * local_rows : (s + 1) * local_rows].astype(bf16)
+            out_buf[s, h] = piece
+
+    def hand_back(h):
+        for p in range(1, groups):
+            o_copy(p, h).start()
+
+    def close(h):
+        finish(h)
+
+        @pl.when(h >= 1)
+        def _():
+            hand_back(h - 1)
 
     @pl.when(core == 1)
     def _():
@@ -333,6 +420,11 @@
 
         def one(h, inner):
             absorb(h, [(at, 1), (at, 0)])
+
+            @pl.when(at == 0)
+            def _():
+                close(h)
+
             return inner
 
         lax.fori_loop(0, heads, one, 0)
@@ -351,14 +443,16 @@
 
     lax.fori_loop(0, level, far, 0)
 
-    def finish(h, carry):
-        out = acc[h] / total[h]
-        n = rows // groups
-        for s in range(groups):
-            o_ref[s, h] = out[s * n : (s + 1) * n].astype(bf16)
-        return carry
-
-    lax.fori_loop(0, heads, finish, 0)
+    @pl.when(level == 0)
+    def _():
+        def last(h, carry):
+            close(h)
+            return carry
+
+        lax.fori_loop(0, heads, last, 0)
+
+    o_ref[me] = out_buf[me]
+    hand_back(heads - 1)
 
     def settle(at, kind, target, send):
         copy(slot(at, core, kind), at, kind, target, send).wait_send()
@@ -395,6 +489,17 @@
         lax.fori_loop(0, level + 1, settle_next, 0)
 
     swap.wait_send()
+    for p in range(1, groups):
+        b_copy(p).wait_send()
+        v_copy(p).wait_send()
+        for c in range(chunks):
+            x_copy(p, c).wait_send()
+
+        def handed(h, carry):
+            o_copy(p, h).wait()
+            return carry
+
+        lax.fori_loop(0, heads, handed, 0)
 
 
 def shards(queries, key_vectors, values, directions, beta_logit):
@@ -407,21 +512,23 @@
     def outgoing(x):
         return x.reshape(local_rows, groups, heads, width).transpose(1, 2, 0, 3)
 
-    stacked = jnp.stack([outgoing(x) for x in (queries, key_vectors, values, directions)], axis=2)
-    arrived = lax.all_to_all(stacked, "head", 0, 0, tiled=True)
-    logit = beta_logit.reshape(local_rows, groups, heads).transpose(1, 2, 0)
-    logit = lax.all_to_all(logit, "head", 0, 0, tiled=True)
-    logit = logit.transpose(1, 0, 2).reshape(heads, 1, rows)
-    value_rows = arrived[:, :, 2].transpose(1, 0, 2, 3).reshape(heads, rows, width)
+    stacked = jnp.stack([outgoing(x) for x in (queries, key_vectors, directions)], axis=2)
+    value_rows = outgoing(values)
+    logit = beta_logit.reshape(local_rows, groups, heads).transpose(1, 2, 0).astype(f32)
+    chunks = 4 if heads % 4 == 0 else heads
     part = heads // 2
     vmem = pl.BlockSpec(memory_space=pltpu.VMEM)
     out = pl.pallas_call(
-        functools.partial(block_kernel, groups, levels, 2 * SUB),
+        functools.partial(block_kernel, groups, levels, 2 * SUB, chunks),
         in_specs=[vmem] * 3,
         out_specs=vmem,
         out_shape=jax.ShapeDtypeStruct((groups, heads, local_rows, width), bf16),
         scratch_shapes=[
-            pltpu.VMEM((levels, 2, 2, heads, rows, width), bf16),
+            pltpu.VMEM(stacked.shape, bf16),
+            pltpu.VMEM(logit.shape, f32),
+            pltpu.VMEM((groups, heads, local_rows, width), bf16),
+            pltpu.VMEM((levels, 2, heads, rows, width), bf16),
+            pltpu.VMEM((levels, 2, heads, groups, local_rows, width), bf16),
             pltpu.VMEM((levels, 2, part, width, width), f32),
             pltpu.VMEM((heads, rows, width), bf16),
             pltpu.VMEM((heads, rows, width), f32),
@@ -436,12 +543,20 @@
             pltpu.SemaphoreType.DMA((levels, 2, 3)),
             pltpu.SemaphoreType.DMA,
             pltpu.SemaphoreType.DMA,
+            pltpu.SemaphoreType.DMA((groups, chunks)),
+            pltpu.SemaphoreType.DMA((groups, chunks)),
+            pltpu.SemaphoreType.DMA((groups,)),
+            pltpu.SemaphoreType.DMA((groups,)),
+            pltpu.SemaphoreType.DMA((groups,)),
+            pltpu.SemaphoreType.DMA((groups,)),
+            pltpu.SemaphoreType.DMA((groups, heads)),
+            pltpu.SemaphoreType.DMA((groups, heads)),
+            pltpu.SemaphoreType.DMA((3,)),
         ],
         compiler_params=pltpu.CompilerParams(collective_id=0, has_side_effects=True),
         name="block_chain",
-    )(arrived, value_rows, logit)
-    back = lax.all_to_all(out, "head", 0, 0, tiled=True)
-    return back.transpose(2, 0, 1, 3).reshape(local_rows, head_total, width)
+    )(stacked, value_rows, logit)
+    return out.transpose(2, 0, 1, 3).reshape(local_rows, head_total, width)
 
 
 def solution(mesh):

time: 196 us -> 163 us (0.83)
  waiting for transfers between devices: 34.3 us -> 0 us
  Pallas kernels: 128 us -> 154 us
  blocking collectives: 14.5 us -> 0 us
  starting transfers between devices: 8.57 us -> 0 us
    all_to_all x2 -> x0, waiting for transfers between devices: 34.3 us -> none  [the longest x1 34.3 us: shards(): arrived = lax.all_to_all(stacked, 'head', 0, 0, tiled=True)]
    pallas_call x1, Pallas kernels: 128 us -> 154 us  [shards(): pl.pallas_call(functools.partial(block_kernel, groups, levels, 2 * SUB, c...]
    all_to_all x1 -> x0, blocking collectives: 14.5 us -> none  [shards(): back = lax.all_to_all(out, 'head', 0, 0, tiled=True)]
    all_to_all x2 -> x0, starting transfers between devices: 8.57 us -> none  [the longest x1 4.38 us: shards(): logit = lax.all_to_all(logit, 'head', 0, 0, tiled=True)]
  transfers between devices with their start and end apart: 2 -> 0, of which waited for: 1 -> 0; matrix products, arithmetic and copies ran while one was open for 3% -> 0% of each run, Pallas kernels for 0% -> 0%
where the time goes in v3:
time: 163 us
  Pallas kernels  154 us (94%)
  local copies, waits for them, and re-layouts  6.78 us (4%)
  other arithmetic  2.26 us (1%)
    pallas_call x1, Pallas kernels, shards(): pl.pallas_call(functools.partial(block_kernel, groups, levels, 2 * SUB, c...  154 us
    unnamed x10, local copies, waits for them, and re-layouts  4.46 us

profile of v3, /device:TPU:26, one launch (start us, length us, event | category | flops | bytes accessed | tf_op | source)
XLA Modules:
  0.0 162.6 jit_solution(1770340420425217605)
XLA Ops:
  0.0 0.0 copy-start
  0.0 1.5 copy.6
  1.5 1.4 copy.7
  3.0 0.0 copy-done
  3.0 0.3 copy.8
  3.3 0.0 copy-start.1
  3.3 0.0 copy-start.2
  3.3 1.7 %pad_maximum_fusion.x_ref = bf16[4,8,3,96,128]{4,3,2,1,0:T(8,128)(2,1)} fusion(bf16[4,8,1,96,128]{4,3,2,1,0:T(8,128)(2,1)S(1)} %bitcast.28, bf16[4,8,1,96,128]{4,3,2,1,0:T(8,128)(2,1)S(1)} %bitcast.27, bf16[4,8,1,96,128]{4,3,2,1,0:T(8,128)(2,1)S(1)} %bitcast.26), kind=kLoop, calls=%fused_computation | loop fusion | flops 2359296 | bytes 4718592 | tf_op jit(solution)/shard_map/stack | solution.py:515
  5.0 0.0 copy-done.1
  5.0 1.2 copy.9
  6.2 0.0 copy-done.2
  6.2 0.6 convert_bitcast_fusion.logit_ref
  6.8 153.5 %block_chain.1 = bf16[4,8,96,128]{3,2,1,0:T(8,128)(2,1)} custom-call(bf16[4,8,3,96,128]{4,3,2,1,0:T(8,128)(2,1)} %pad_maximum_fusion.x_ref, bf16[4,8,96,128]{3,2,1,0:T(8,128)(2,1)} %bitcast.30, f32[4,8,96]{2,1,0:T(8,128)} %convert_bitcast_fusion.logit_ref), custom_call_target="tpu_custom_call" | custom-call | tf_op jit(solution)/shard_map/block_chain/pallas_call | solution.py:521
  160.3 2.3 %copy.10 = bf16[96,32,128]{2,1,0:T(8,128)(2,1)} copy(bf16[96,32,128]{2,0,1:T(8,128)(2,1)} %bitcast.29) | data formatting | bytes 1572864 | tf_op jit(solution)/shard_map/reshape | solution.py:559
Async XLA Ops:
  0.0 3.0 %copy-start = (bf16[96,32,128]{2,1,0:T(8,128)(2,1)S(1)}, bf16[96,32,128]{2,1,0:T(8,128)(2,1)}, u32[]{:S(2)}) copy-start(bf16[96,32,128]{2,1,0:T(8,128)(2,1)} %param.8) | copy-start | bytes 2359300
  3.3 1.7 %copy-start.1 = (bf16[96,32,128]{2,1,0:T(8,128)(2,1)S(1)}, bf16[96,32,128]{2,1,0:T(8,128)(2,1)}, u32[]{:S(2)}) copy-start(bf16[96,32,128]{2,1,0:T(8,128)(2,1)} %param.7) | copy-start | bytes 2359300
  3.3 2.9 %copy-start.2 = (bf16[96,32]{0,1:T(8,128)(2,1)S(1)}, bf16[96,32]{0,1:T(8,128)(2,1)}, u32[]{:S(2)}) copy-start(bf16[96,32]{0,1:T(8,128)(2,1)} %param.9) | copy-start | bytes 18436

commit v4 on v3

--- a/solution.py
+++ b/solution.py
@@ -135,7 +135,7 @@
     )
 
 
-KEYS, VALUES, MAPS = 0, 1, 2
+VALUES, MAPS, KEYS = 0, 1, 2
 MESH = pl.DeviceIdType.MESH
 
 
@@ -234,7 +234,9 @@
         return jnp.concatenate(pieces, axis=0).astype(bf16)
 
     def slot(at, column, kind):
-        return (key_buf, value_buf, map_buf)[kind].at[at, column]
+        if isinstance(kind, int) and kind < KEYS:
+            return (value_buf, map_buf)[kind].at[at, column]
+        return key_buf.at[at, column, pl.ds((kind - KEYS) * chunk, chunk)]
 
     def copy(source, at, kind, target, send):
         return pltpu.make_async_remote_copy(
@@ -303,11 +305,22 @@
         for p in range(1, groups):
             x_copy(p, c).wait_recv()
         lax.fori_loop(c * chunk, (c + 1) * chunk, local, 0)
-        if c == (chunks - 1) // 2:
+
+        @pl.when((core == 1) & has_next)
+        def _():
+            send_next(key_self.at[pl.ds(c * chunk, chunk)], level, KEYS + c)
+
+        if c == 0:
 
             @pl.when(level >= 1)
             def _():
                 relay(level - 1, VALUES)
+
+        if c == min(2, chunks - 1):
+
+            @pl.when(level >= 2)
+            def _():
+                relay(level - 2, VALUES)
 
     swap = pltpu.make_async_remote_copy(
         src_ref=own_map,
@@ -319,17 +332,11 @@
     )
     swap.start()
 
-    @pl.when((core == 1) & has_next)
-    def _():
-        send_next(key_self, level, KEYS)
-
     @pl.when(core == 0)
     def _():
-        copy(key_self, level, KEYS, side, send_side).start()
-
-    @pl.when(level >= 2)
-    def _():
-        relay(level - 2, VALUES)
+        for c in range(chunks):
+            source = key_self.at[pl.ds(c * chunk, chunk)]
+            copy(source, level, KEYS + c, side, send_side).start()
 
     swap.wait_recv()
 
@@ -339,8 +346,11 @@
             key_buf[level, 0, h] = wide_nt(key_wide[h], side_map[h]).astype(bf16)
             return carry
 
-        lax.fori_loop(0, heads, rebase, 0)
-        send_next(slot(level, 0, KEYS), level, KEYS)
+        for c in range(chunks):
+            lax.fori_loop(c * chunk, (c + 1) * chunk, rebase, 0)
+            if c >= 1:
+                send_next(slot(level, 0, KEYS + c - 1), level, KEYS + c - 1)
+        send_next(slot(level, 0, KEYS + chunks - 1), level, KEYS + chunks - 1)
 
     @pl.when(has_map & (core == 0))
     def _():
@@ -393,7 +403,8 @@
     @pl.when(core == 1)
     def _():
         await_slot(level, 0, VALUES)
-        await_slot(level, 0, KEYS)
+        for c in range(chunks):
+            await_slot(level, 0, KEYS + c)
 
         def near(h, carry):
             absorb(h, [(level, 0)])
@@ -409,14 +420,12 @@
         def _():
             relay(at, VALUES)
 
-        relay(at, KEYS)
-
-        @pl.when(at >= 1)
-        def _():
-            relay(at, MAPS)
-
         await_slot(at, 1 - core, VALUES)
-        await_slot(at, 1 - core, KEYS)
+
+        def some(c, inner):
+            relay(at, KEYS + c)
+            await_slot(at, 1 - core, KEYS + c)
+            return lax.fori_loop(c * chunk, (c + 1) * chunk, one, inner)
 
         def one(h, inner):
             absorb(h, [(at, 1), (at, 0)])
@@ -427,7 +436,11 @@
 
             return inner
 
-        lax.fori_loop(0, heads, one, 0)
+        lax.fori_loop(0, chunks, some, 0)
+
+        @pl.when(at >= 1)
+        def _():
+            relay(at, MAPS)
 
         @pl.when(at >= 1)
         def _():
@@ -458,7 +471,8 @@
         copy(slot(at, core, kind), at, kind, target, send).wait_send()
 
     def settle_side(at, carry):
-        settle(at, KEYS, side, send_side)
+        for c in range(chunks):
+            settle(at, KEYS + c, side, send_side)
         settle(at, VALUES, side, send_side)
 
         @pl.when(at >= 1)
@@ -468,7 +482,8 @@
         return carry
 
     def settle_next(at, carry):
-        settle(at, KEYS, onward, send_on)
+        for c in range(chunks):
+            settle(at, KEYS + c, onward, send_on)
         settle(at, VALUES, onward, send_on)
 
         @pl.when(at >= 1)
@@ -481,7 +496,8 @@
 
     @pl.when(core == 0)
     def _():
-        settle(level, KEYS, side, send_side)
+        for c in range(chunks):
+            settle(level, KEYS + c, side, send_side)
         settle(level, VALUES, side, send_side)
 
     @pl.when(has_next)
@@ -538,9 +554,9 @@
             pltpu.VMEM((heads, rows, 1), f32),
             pltpu.VMEM((heads, width, width), f32),
             pltpu.VMEM((heads, width, width), f32),
-            pltpu.SemaphoreType.DMA((levels, 3)),
-            pltpu.SemaphoreType.DMA((levels, 3)),
-            pltpu.SemaphoreType.DMA((levels, 2, 3)),
+            pltpu.SemaphoreType.DMA((levels, KEYS + chunks)),
+            pltpu.SemaphoreType.DMA((levels, KEYS + chunks)),
+            pltpu.SemaphoreType.DMA((levels, 2, KEYS + chunks)),
             pltpu.SemaphoreType.DMA,
             pltpu.SemaphoreType.DMA,
             pltpu.SemaphoreType.DMA((groups, chunks)),

time: 163 us -> 151 us (0.926)
  Pallas kernels: 154 us -> 141 us
    pallas_call x1, Pallas kernels: 154 us -> 141 us  [shards(): pl.pallas_call(functools.partial(block_kernel, groups, levels, 2 * SUB, c...]
where the time goes in v4:
time: 151 us; the launch traced here: 150 us
  Pallas kernels  141 us (93%)
  local copies, waits for them, and re-layouts  6.78 us (4%)
  other arithmetic  2.26 us (1%)
    pallas_call x1, Pallas kernels, shards(): pl.pallas_call(functools.partial(block_kernel, groups, levels, 2 * SUB, c...  141 us
    unnamed x10, local copies, waits for them, and re-layouts  4.46 us

profile of v4, /device:TPU:26, one launch (start us, length us, event | category | flops | bytes accessed | tf_op | source)
XLA Modules:
  0.0 150.5 jit_solution(2731276668300334089)
XLA Ops:
  0.0 0.0 copy-start
  0.0 1.5 %copy.6 = bf16[96,32,128]{2,0,1:T(8,128)(2,1)S(1)} copy(bf16[96,32,128]{2,1,0:T(8,128)(2,1)} %param.5) | data formatting | bytes 1572864 | tf_op args[0]
  1.5 1.4 copy.7
  3.0 0.0 copy-done
  3.0 0.3 copy.8
  3.3 0.0 copy-start.1
  3.3 0.0 copy-start.2
  3.3 1.7 %pad_maximum_fusion.x_ref = bf16[4,8,3,96,128]{4,3,2,1,0:T(8,128)(2,1)} fusion(bf16[4,8,1,96,128]{4,3,2,1,0:T(8,128)(2,1)S(1)} %bitcast.28, bf16[4,8,1,96,128]{4,3,2,1,0:T(8,128)(2,1)S(1)} %bitcast.27, bf16[4,8,1,96,128]{4,3,2,1,0:T(8,128)(2,1)S(1)} %bitcast.26), kind=kLoop, calls=%fused_computation | loop fusion | flops 2359296 | bytes 4718592 | tf_op jit(solution)/shard_map/stack | solution.py:531
  5.0 0.0 copy-done.1
  5.0 1.2 copy.9
  6.2 0.0 copy-done.2
  6.2 0.6 convert_bitcast_fusion.logit_ref
  6.8 141.4 %block_chain.1 = bf16[4,8,96,128]{3,2,1,0:T(8,128)(2,1)} custom-call(bf16[4,8,3,96,128]{4,3,2,1,0:T(8,128)(2,1)} %pad_maximum_fusion.x_ref, bf16[4,8,96,128]{3,2,1,0:T(8,128)(2,1)} %bitcast.30, f32[4,8,96]{2,1,0:T(8,128)} %convert_bitcast_fusion.logit_ref), custom_call_target="tpu_custom_call" | custom-call | tf_op jit(solution)/shard_map/block_chain/pallas_call | solution.py:537
  148.2 2.3 %copy.10 = bf16[96,32,128]{2,1,0:T(8,128)(2,1)} copy(bf16[96,32,128]{2,0,1:T(8,128)(2,1)} %bitcast.29) | data formatting | bytes 1572864 | tf_op jit(solution)/shard_map/reshape | solution.py:575
Async XLA Ops:
  0.0 3.0 %copy-start = (bf16[96,32,128]{2,1,0:T(8,128)(2,1)S(1)}, bf16[96,32,128]{2,1,0:T(8,128)(2,1)}, u32[]{:S(2)}) copy-start(bf16[96,32,128]{2,1,0:T(8,128)(2,1)} %param.8) | copy-start | bytes 2359300
  3.3 1.7 %copy-start.1 = (bf16[96,32,128]{2,1,0:T(8,128)(2,1)S(1)}, bf16[96,32,128]{2,1,0:T(8,128)(2,1)}, u32[]{:S(2)}) copy-start(bf16[96,32,128]{2,1,0:T(8,128)(2,1)} %param.7) | copy-start | bytes 2359300
  3.3 2.9 %copy-start.2 = (bf16[96,32]{0,1:T(8,128)(2,1)S(1)}, bf16[96,32]{0,1:T(8,128)(2,1)}, u32[]{:S(2)}) copy-start(bf16[96,32]{0,1:T(8,128)(2,1)} %param.9) | copy-start | bytes 18436
